TPU v7x, 32 devices: a whole 2x2x4 slice. The times are simulated.
32 devices in a mesh: space: 8 (over z, y), step: 4 (over x, core).
Axes of the slice: x: 2, y: 2, z: 4, core: 2. Of those that a mesh axis runs over, the one named last changes fastest.
Arguments:
- image: float32 [3, 128, 256], P(None, 'space'), may hold values from -6 to 6
- baseline: float32 [3, 128, 256], P(None, 'space'), may hold values from -0.5 to 0.5
- w_first: float32 [64, 3, 3, 3], replicated, may hold values from -1.25 to 1.25
- w_rest: float32 [3, 64, 64, 3, 3], replicated, may hold values from -0.375 to 0.375
- target: float32 [64, 128, 256], P(None, 'space'), may hold values from -6 to 6
Outputs:
- attribution: float32 [3, 128, 256], P(None, 'space')
All inputs are finite; a program needn't handle non-finite values.
Results may differ from a plain program's by a relative error of at most 0.0001.
Values sent between devices are 32-bit elements; how exact they have to be, the bound alone decides.
No kernel may reach another device: no remote copies, remote signals or barrier semaphores. Data moves between devices by JAX's collectives and lax.ppermute only.
A program may use at most 64 MiB of HBM per device.

v0:
```python
import jax
import jax.numpy as jnp
from jax import lax
from jax.experimental import pallas as pl
from jax.experimental.pallas import tpu as pltpu
from jax.sharding import PartitionSpec as P

F32, BF16 = jnp.float32, jnp.bfloat16
HALO_X, HALO_T = 6, 4
VMEM = pl.BlockSpec(memory_space=pltpu.VMEM)
SMEM = pl.BlockSpec(memory_space=pltpu.SMEM)


def dot(a, b):
    return jnp.dot(a, b, preferred_element_type=F32)


def split(value):
    high = value.astype(BF16)
    return high, (value - high.astype(F32)).astype(BF16)


def shift_cols(value, by):
    width = value.shape[-1]
    col = lax.broadcasted_iota(jnp.int32, value.shape, value.ndim - 1)
    edge = 0 if by > 0 else width - 1
    return jnp.where(col == edge, 0.0, pltpu.roll(value, by % width, value.ndim - 1))


def combine(y, rows):
    return y[rows : 2 * rows] + shift_cols(y[:rows], 1) + shift_cols(y[2 * rows : 3 * rows], -1)


def silu_and_slope(pre):
    sig = 1.0 / (1.0 + jnp.exp(-pre))
    act = pre * sig
    return act, sig + act * (1.0 - sig)


def conv_row(weights, high, low, index):
    stack = lambda ref: ref[index : index + 3].reshape(3 * ref.shape[1], ref.shape[2])
    upper, lower = stack(high), stack(low)
    return dot(weights, jnp.concatenate([upper, upper, lower], 0))


class Maps:
    def __init__(self, refs, base):
        self.high, self.low = refs
        self.base = base

    def put(self, step, row, value):
        self.high[step, row - self.base], self.low[step, row - self.base] = split(value)

    def conv(self, weights, step, row):
        return conv_row(weights, self.high.at[step], self.low.at[step], row - 1 - self.base)

    def copy(self, refs, row, count):
        for part, ref in zip((self.high, self.low), refs):
            ref[...] = part[:, row - self.base : row - self.base + count]

    def load(self, refs, row, count):
        for part, ref in zip((self.high, self.low), refs):
            part[:, row - self.base : row - self.base + count] = ref[...]


def run(spans, weights, xs, x_base, maps, slopes, x_row, t_row, keep, emit, channels, width):
    w1, wf, wb, w1t = weights
    a1, a2, t, d3, d2, d1 = maps
    s1, s1_base, s2, s2_base = slopes
    rows = lambda name: range(spans[name][0], spans[name][1] + 1)
    inside = lambda name, row: spans[name][0] <= row <= spans[name][1]
    for j in rows("x"):
        x = x_row(j)
        taps = jnp.concatenate([shift_cols(x, 1), x, shift_cols(x, -1)], 0)
        high = taps.astype(BF16).astype(F32)
        xs[j - x_base] = jnp.concatenate([high, taps - high], 0).astype(BF16)
    for j in rows("t"):
        t.put(0, j, t_row(j))
    for j in rows("a1"):
        stack = xs[j - 1 - x_base : j + 2 - x_base].reshape(3 * xs.shape[1], width)
        pre = dot(w1[...], jnp.concatenate([stack, stack], 0))
        for s in range(2):
            act, slope = silu_and_slope(pre[s * channels : (s + 1) * channels])
            a1.put(s, j, keep(act, j))
            if inside("s1", j):
                s1[s, j - s1_base] = keep(slope, j)
    for j in rows("a2"):
        for s in range(2):
            act, slope = silu_and_slope(combine(a1.conv(wf[0], s, j), channels))
            a2.put(s, j, keep(act, j))
            if inside("s2", j):
                s2[s, j - s2_base] = keep(slope, j)
    for j in rows("d3"):
        grad = combine(t.conv(wb[2], 0, j), channels)
        for s in range(2):
            _, slope = silu_and_slope(combine(a2.conv(wf[1], s, j), channels))
            d3.put(s, j, keep(grad * slope, j))
    for j in rows("d2"):
        for s in range(2):
            d2.put(s, j, combine(d3.conv(wb[1], s, j), channels) * s2[s, j - s2_base])
    for j in rows("d1"):
        for s in range(2):
            d1.put(s, j, combine(d2.conv(wb[0], s, j), channels) * s1[s, j - s1_base])
    for j in rows("out"):
        emit(j, combine(d1.conv(w1t[...], 0, j) + d1.conv(w1t[...], 1, j), 8))


def prepare(side, w, w_first, w1, wf, wb, w1t, channels, colours):
    tap = lambda dy: jnp.where(side == 1, 2 - dy, dy)

    def halves(pieces):
        high = [p.astype(BF16).astype(F32) for p in pieces]
        return high, [p - h for p, h in zip(pieces, high)]

    def wide(pieces):
        high, low = halves(pieces)
        return jnp.concatenate(high + low + high, 1).astype(BF16)

    for layer in range(wf.shape[0]):
        for dx in range(3):
            wf[layer, pl.ds(dx * channels, channels), :] = wide([w[layer, tap(dy), dx] for dy in range(3)])
    for layer in range(wb.shape[0]):
        for dx in range(3):
            pieces = [w[layer, tap(2 - dy), 2 - dx].T for dy in range(3)]
            wb[layer, pl.ds(dx * channels, channels), :] = wide(pieces)
    zeros = lambda count: jnp.zeros((count, channels), F32)
    for s in range(2):
        fronts, backs = [], []
        for dy in range(3):
            slots = [
                jnp.concatenate([zeros(4)] * s + [w_first[:, tap(dy), dx, :], zeros(4 - colours)] + [zeros(4)] * (1 - s), 0)
                for dx in range(3)
            ]
            (high,), (low,) = halves([jnp.concatenate(slots, 0)])
            fronts += [high, high]
            backs += [low, jnp.zeros_like(low)]
        w1[pl.ds(s * channels, channels), :] = jnp.concatenate(fronts + backs, 0).T.astype(BF16)
    last = [
        jnp.concatenate(
            sum([[w_first[:, tap(2 - dy), 2 - dx, :], zeros(8 - colours)] for dx in range(3)], []), 0
        )
        for dy in range(3)
    ]
    w1t[...] = wide(last)


def pack_kernel(rows):
    def kernel(side_ref, fractions, image, baseline, target, x_own, send, tile, sem):
        side = side_ref[0]
        channels = target.shape[0]
        start = pl.multiple_of((1 - side) * (rows - 8), 8)
        fetch = pltpu.make_async_copy(target.at[:, pl.ds(start, 8), :], tile, sem)
        fetch.start()
        base, difference = baseline[...], image[...] - baseline[...]
        colours = base.shape[0]
        zero = jnp.zeros((4 - colours,) + base.shape[1:], F32)
        for s in range(2):
            x_own[pl.ds(4 * s, colours)] = base + fractions[s] * difference
            x_own[pl.ds(4 * s + colours, 4 - colours)] = zero
        for j in range(HALO_X):
            row = jnp.where(side == 0, rows - HALO_X + j, HALO_X - 1 - j)
            send[pl.ds(HALO_T * channels + 8 * j, 8), :] = x_own[:, row, :]
        fetch.wait()
        for j in range(HALO_T):
            row = jnp.where(side == 0, 8 - HALO_T + j, HALO_T - 1 - j)
            send[pl.ds(channels * j, channels), :] = tile[:, row, :]

    return kernel


def spans_of(half):
    near = {"x": (-6, 1), "t": (-4, 3), "a1": (-5, 0), "s1": (-1, 0), "a2": (-4, 1), "s2": (-2, 1)}
    near |= {"d3": (-3, 2), "d2": (-2, 3), "d1": (-1, 4), "out": (0, 5)}
    far = {"x": (0, half + 5), "t": (2, half + 3), "a1": (1, half + 4), "s1": (1, half), "a2": (2, half + 3)}
    far |= {"s2": (2, half + 1), "d3": (3, half + 2), "d2": (4, half + 1), "d1": (5, half), "out": (6, half - 1)}
    return near, far


def far_kernel(rows, half, channels, width):
    def kernel(side_ref, x_own, target, w, w_first, *refs):
        w1, wf, wb, w1t, out = refs[:5]
        edges, (e1, e2) = refs[5:15], refs[15:17]
        xs, s1, s2 = refs[17:20]
        work = refs[20:]
        side = side_ref[0]
        row_of = lambda local: jnp.where(side == 0, local, rows - 1 - local)
        prepare(side, w, w_first, w1, wf, wb, w1t, channels, x_colours(w_first))
        spans = spans_of(half)[1]
        maps = [Maps(work[2 * i : 2 * i + 2], b) for i, b in enumerate((1, 2, 2, 3, 4, 5))]

        def emit(j, value):
            out[j - spans["out"][0]] = value

        run(
            spans, (w1, wf, wb, w1t), xs, 0, maps, (s1, 1, s2, 2),
            lambda j: x_own[:, row_of(j), :], lambda j: target[:, row_of(j), :],
            lambda value, j: value, emit, channels, width,
        )
        a1, a2, _, d3, d2, d1 = maps
        for i, (m, row) in enumerate(((a1, 1), (a2, 2), (d3, 3), (d2, 4), (d1, 5))):
            m.copy(edges[2 * i : 2 * i + 2], row, 2)
        e1[...] = s1[:, 0:4]
        e2[...] = s2[:, 0:2]

    return kernel


def x_colours(w_first):
    return w_first.shape[0]


def near_kernel(rows, half, channels, width):
    def kernel(info, x_own, target, halo, *refs):
        w1, wf, wb, w1t, far_out = refs[:5]
        edges, (e1, e2) = refs[5:15], refs[15:17]
        out = refs[17]
        xs, s1, s2 = refs[18:21]
        work = refs[21:]
        side, exists = info[0], info[1] == 1
        row_of = lambda local: jnp.where(side == 0, local, rows - 1 - local)
        place = lambda local: jnp.where(side == 0, local, half - 1 - local)
        spans = spans_of(half)[0]
        maps = [Maps(work[2 * i : 2 * i + 2], b) for i, b in enumerate((-5, -4, -4, -3, -2, -1))]
        a1, a2, _, d3, d2, d1 = maps
        for i, (m, row) in enumerate(((a1, 1), (a2, 2), (d3, 3), (d2, 4), (d1, 5))):
            m.load(edges[2 * i : 2 * i + 2], row, 2)
        s1[:, 2:6] = e1[...]
        s2[:, 4:6] = e2[...]
        for j in range(6, half):
            out[place(j)] = far_out[j - 6]

        def x_row(j):
            if j < 0:
                return halo[pl.ds(HALO_T * channels + 8 * (j + HALO_X), 8), :]
            return x_own[:, row_of(j), :]

        def t_row(j):
            if j < 0:
                return halo[pl.ds(channels * (j + HALO_T), channels), :]
            return target[:, row_of(j), :]

        def keep(value, j):
            return jnp.where(exists, value, 0.0) if j < 0 else value

        def emit(j, value):
            out[place(j)] = value

        run(
            spans, (w1, wf, wb, w1t), xs, -6, maps, (s1, -1, s2, -2),
            x_row, t_row, keep, emit, channels, width,
        )

    return kernel


def body(image, baseline, w_first, w_rest, target):
    colours, rows, width = image.shape
    channels = target.shape[0]
    half = rows // 2
    space_n, step_n = lax.axis_size("space"), lax.axis_size("step")
    space, step = lax.axis_index("space"), lax.axis_index("step")
    side, group = step % 2, step // 2
    first = (group * 2).astype(F32) + 0.5
    fractions = jnp.stack([first / step_n, (first + 1.0) / step_n])
    exists = jnp.where(side == 0, space > 0, space < space_n - 1)
    info = jnp.stack([side, exists.astype(jnp.int32)]).astype(jnp.int32)
    params = pltpu.CompilerParams(vmem_limit_bytes=40 << 20)
    shape = jax.ShapeDtypeStruct

    x_own, send = pl.pallas_call(
        pack_kernel(rows),
        out_shape=(shape((8, rows, width), F32), shape((HALO_T * channels + HALO_X * 8, width), F32)),
        in_specs=[SMEM, SMEM, VMEM, VMEM, pl.BlockSpec(memory_space=pl.ANY)],
        out_specs=(VMEM, VMEM),
        scratch_shapes=[pltpu.VMEM((channels, 8, width), F32), pltpu.SemaphoreType.DMA(())],
        compiler_params=params,
        name="pack_edges",
    )(info, fractions, image, baseline, target)

    pairs = []
    for i in range(space_n):
        for s in range(step_n):
            source = i + 1 if s % 2 else i - 1
            if 0 <= source < space_n:
                pairs.append((source * step_n + s, i * step_n + s))
    halo = lax.ppermute(send, ("space", "step"), pairs)

    n = 3 * channels
    weight_shapes = [
        shape((2 * channels, 288), BF16),
        shape((2, n, 3 * n), BF16),
        shape((3, n, 3 * n), BF16),
        shape((24, 3 * n), BF16),
    ]
    edge_shapes = [shape((2, 2, channels, width), BF16)] * 10
    edge_shapes += [shape((2, 4, channels, width), F32), shape((2, 2, channels, width), F32)]

    def scratch(x_rows, s1_rows, s2_rows, counts):
        refs = [pltpu.VMEM((x_rows, 48, width), BF16)]
        refs += [pltpu.VMEM((2, r, channels, width), F32) for r in (s1_rows, s2_rows)]
        for i, count in enumerate(counts):
            refs += [pltpu.VMEM((1 if i == 2 else 2, count, channels, width), BF16)] * 2
        return refs

    far = pl.pallas_call(
        far_kernel(rows, half, channels, width),
        out_shape=(*weight_shapes, shape((half - 6, 8, width), F32), *edge_shapes),
        in_specs=[SMEM] + [VMEM] * 4,
        out_specs=(VMEM,) * 17,
        scratch_shapes=scratch(half + 6, half, half, (half + 4, half + 2, half + 2, half, half - 2, half - 4)),
        compiler_params=params,
        name="far_rows",
    )(info, x_own, target, w_rest.transpose(0, 3, 4, 1, 2), w_first.transpose(1, 2, 3, 0))

    y = pl.pallas_call(
        near_kernel(rows, half, channels, width),
        out_shape=shape((half, 8, width), F32),
        in_specs=[SMEM] + [VMEM] * 20,
        out_specs=VMEM,
        scratch_shapes=scratch(8, 6, 6, (8,) * 6),
        compiler_params=params,
        name="near_rows",
    )(info, x_own, target, halo, *far)
    y = y.transpose(1, 0, 2)[:colours]

    def partner(k):
        return lax.ppermute(y, "step", [(i, i ^ k) for i in range(step_n)])

    difference = image - baseline
    if step_n == 4:
        mine, theirs = y + partner(2), partner(1) + partner(3)
        whole = jnp.where(side == 0, jnp.concatenate([mine, theirs], 1), jnp.concatenate([theirs, mine], 1))
    else:
        order = lax.broadcasted_iota(jnp.int32, (2, 1, 1, 1), 0)
        halves = lax.psum(jnp.where(order == side, y[None], 0.0), "step")
        whole = jnp.concatenate([halves[0], halves[1]], 1)
    return difference * whole / step_n


def solution(mesh):
    in_specs = (P(None, "space", None), P(None, "space", None), P(), P(), P(None, "space", None))
    out_specs = P(None, "space", None)
    return jax.shard_map(body, mesh=mesh, in_specs=in_specs, out_specs=out_specs, check_vma=False)
```

profile of v0, /device:TPU:0, one launch (start us, length us, event | category | flops | bytes accessed | tf_op | source)
XLA Modules:
  0.0 30.9 jit_solution(4750224151497147336)
XLA Ops:
  0.0 0.0 copy-start.3
  0.0 0.1 pad_add_fusion.side_ref.info
  0.1 0.1 pad_maximum_fusion.fractions
  0.2 0.6 %copy-done.3 = f32[3,16,256]{2,1,0:T(8,128)S(1)} copy-done((f32[3,16,256]{2,1,0:T(8,128)S(1)}, f32[3,16,256]{2,1,0:T(8,128)}, u32[]{:S(2)}) %copy-start.3) | copy-done | bytes 49176
  0.8 1.2 %copy-done = f32[64,16,256]{2,1,0:T(8,128)S(1)} copy-done((f32[64,16,256]{2,1,0:T(8,128)S(1)}, f32[64,16,256]{2,1,0:T(8,128)}, u32[]{:S(2)}) %copy-start) | copy-done | bytes 1048600
  2.0 0.8 %copy-done.4 = f32[3,16,256]{2,1,0:T(8,128)S(1)} copy-done((f32[3,16,256]{2,1,0:T(8,128)S(1)}, f32[3,16,256]{2,1,0:T(8,128)}, u32[]{:S(2)}) %copy-start.4) | copy-done | bytes 49176
  2.8 0.8 %pack_edges.1 = (f32[8,16,256]{2,1,0:T(8,128)S(1)}, f32[304,256]{1,0:T(8,128)S(1)}) custom-call(s32[2]{0:T(128)S(1)} %pad_add_fusion.side_ref.info, f32[2]{0:T(128)S(1)} %pad_maximum_fusion.fractions, f32[3,16,256]{2,1,0:T(8,128)S(1)} %copy-done.3, f32[3,16,256]{2,1,0:T(8,128)S(1)} %copy-done.4, f32[64,16,256]{2,1,0:T(8,128)S(1)} %copy-done), custom_call_target="tpu_custom_call" | custom-call | tf_op jit(solution)/shard_map/pack_edges/pallas_call | solution.py:270
  3.6 4.9 %collective-permute-start = (f32[304,256]{1,0:T(8,128)S(1)}, f32[304,256]{1,0:T(8,128)S(1)}, u32[]{:S(2)}, u32[]{:S(2)}) collective-permute-start(f32[304,256]{1,0:T(8,128)S(1)} %get-tuple-element.25), channel_id=1, source_target_pairs={{5,1},{7,3},{0,4},{9,5},{2,6},{11,7},{4,8},{13,9},{6,10},{15,11},{... | collective-permute-start | bytes 933896 | tf_op jit(solution)/shard_map/ppermute | solution.py:286
  8.5 0.0 copy-done.1
  8.5 0.0 copy-done.6
  8.5 0.0 copy-start.2
  8.5 1.2 %copy-done.2 = f32[3,64,64,3,3]{2,1,4,3,0:T(8,128)S(1)} copy-done((f32[3,64,64,3,3]{2,1,4,3,0:T(8,128)S(1)}, f32[3,64,64,3,3]{2,1,4,3,0:T(8,128)}, u32[]{:S(2)}) %copy-start.2) | copy-done | bytes 442392
  9.7 8.7 %far_rows.1 = (bf16[128,288]{1,0:T(8,128)(2,1)S(1)}, bf16[2,192,576]{2,1,0:T(8,128)(2,1)S(1)}, bf16[3,192,576]{2,1,0:T(8,128)(2,1)S(1)}, bf16[24,576]{1,0:T(8,12...) custom-call(s32[2]{0:T(128)S(1)} %pad_add_fusion.side_ref.info, ...), custom_call_target="tpu_custom_call" | custom-call | tf_op jit(solution)/shard_map/far_rows/pallas_call | solution.py:305
  18.4 0.0 collective-permute-done.halo
  18.4 6.7 %near_rows.1 = f32[8,8,256]{2,1,0:T(8,128)S(1)} custom-call(s32[2]{0:T(128)S(1)} %pad_add_fusion.side_ref.info, f32[8,16,256]{2,1,0:T(8,128)S(1)} %get-tuple-element.24.x_own, f32[64,16,256]{2,1,0:T(8,128)S(1)} %copy-done.1, f32[304,256]{1,0:T(8,128)S(1)} %collective-permute-done.halo, bf16[128,288]{1,0:T(8,128)(2,1)S(1)} %get-tuple-element.26.refs_0_, ...), custom_call_target="tpu_custom_call" | custom-call | tf_op jit(solution)/shard_map/near_rows/pallas_call | solution.py:315
  25.2 1.6 %collective-permute-start.1 = (f32[3,8,256]{2,0,1:T(4,128)S(1)}, f32[3,8,256]{2,0,1:T(4,128)S(1)}, u32[]{:S(2)}, u32[]{:S(2)}) collective-permute-start(f32[3,8,256]{2,0,1:T(4,128)S(1)} %slice.4), channel_id=1, source_target_pairs={{0,2},{1,3},{2,0},{3,1},{4,6},{5,7},{6,4},{7,5},{8,10},{9,11},{10,... | collective-permute-start | bytes 73736 | tf_op jit(solution)/shard_map/ppermute | solution.py:327
  26.7 0.0 copy-done.5
  26.8 0.1 collective-permute-start.2
  26.8 0.8 %collective-permute-start.3 = (f32[3,8,256]{2,0,1:T(4,128)S(1)}, f32[3,8,256]{2,0,1:T(4,128)S(1)}, u32[]{:S(2)}, u32[]{:S(2)}) collective-permute-start(f32[3,8,256]{2,0,1:T(4,128)S(1)} %slice.4), channel_id=1, source_target_pairs={{0,3},{1,2},{2,1},{3,0},{4,7},{5,6},{6,5},{7,4},{8,11},{9,10},{10,... | collective-permute-start | bytes 73736 | tf_op jit(solution)/shard_map/ppermute | solution.py:327
  27.7 1.5 %collective-permute-done.1 = f32[3,8,256]{2,0,1:T(4,128)S(1)} collective-permute-done((f32[3,8,256]{2,0,1:T(4,128)S(1)}, f32[3,8,256]{2,0,1:T(4,128)S(1)}, u32[]{:S(2)}, u32[]{:S(2)}) %collective-permute-start.1) | collective-permute-done | bytes 24608 | tf_op jit(solution)/shard_map/ppermute | solution.py:327
  29.2 0.0 collective-permute-done.2
  29.2 1.1 %collective-permute-done.3 = f32[3,8,256]{2,0,1:T(4,128)S(1)} collective-permute-done((f32[3,8,256]{2,0,1:T(4,128)S(1)}, f32[3,8,256]{2,0,1:T(4,128)S(1)}, u32[]{:S(2)}, u32[]{:S(2)}) %collective-permute-start.3) | collective-permute-done | bytes 24608 | tf_op jit(solution)/shard_map/ppermute | solution.py:327
  30.3 0.1 fusion.1
  30.3 0.6 %copy.10 = f32[3,16,256]{2,1,0:T(8,128)} copy(f32[3,16,256]{2,0,1:T(4,128)S(1)} %fusion.1) | data formatting | bytes 98304 | tf_op jit(solution)/shard_map/div | solution.py:337
  (9 shorter events, 0.1 us)
Async XLA Ops:
  0.0 0.8 %copy-start.3 = (f32[3,16,256]{2,1,0:T(8,128)S(1)}, f32[3,16,256]{2,1,0:T(8,128)}, u32[]{:S(2)}) copy-start(f32[3,16,256]{2,1,0:T(8,128)} %image.1) | copy-start | bytes 147460
  0.8 1.2 %copy-start = (f32[64,16,256]{2,1,0:T(8,128)S(1)}, f32[64,16,256]{2,1,0:T(8,128)}, u32[]{:S(2)}) copy-start(f32[64,16,256]{2,1,0:T(8,128)} %target.5) | copy-start | bytes 3145732
  2.0 0.8 %copy-start.4 = (f32[3,16,256]{2,1,0:T(8,128)S(1)}, f32[3,16,256]{2,1,0:T(8,128)}, u32[]{:S(2)}) copy-start(f32[3,16,256]{2,1,0:T(8,128)} %baseline.1) | copy-start | bytes 147460
  2.8 5.7 %copy-start.1 = (f32[64,16,256]{2,1,0:T(8,128)S(1)}, f32[64,16,256]{2,1,0:T(8,128)}, u32[]{:S(2)}) copy-start(f32[64,16,256]{2,1,0:T(8,128)} %target.5) | copy-start | bytes 3145732
  2.8 5.7 %copy-start.6 = (f32[64,3,3,3]{0,3,2,1:T(4,128)S(1)}, f32[64,3,3,3]{0,3,2,1:T(4,128)}, u32[]{:S(2)}) copy-start(f32[64,3,3,3]{0,3,2,1:T(4,128)} %param.7) | copy-start | bytes 20740
  3.6 14.8 %collective-permute-start = (f32[304,256]{1,0:T(8,128)S(1)}, f32[304,256]{1,0:T(8,128)S(1)}, u32[]{:S(2)}, u32[]{:S(2)}) collective-permute-start(f32[304,256]{1,0:T(8,128)S(1)} %get-tuple-element.25), channel_id=1, source_target_pairs={{5,1},{7,3},{0,4},{9,5},{2,6},{11,7},{4,8},{13,9},{6,10},{15,11},{... | collective-permute-start | bytes 933896 | tf_op jit(solution)/shard_map/ppermute | solution.py:286
  8.5 1.2 %copy-start.2 = (f32[3,64,64,3,3]{2,1,4,3,0:T(8,128)S(1)}, f32[3,64,64,3,3]{2,1,4,3,0:T(8,128)}, u32[]{:S(2)}) copy-start(f32[3,64,64,3,3]{2,1,4,3,0:T(8,128)} %param.8) | copy-start | bytes 1327108
  25.1 1.6 %copy-start.5 = (f32[3,16,256]{2,1,0:T(8,128)S(1)}, f32[3,16,256]{2,1,0:T(8,128)}, u32[]{:S(2)}) copy-start(f32[3,16,256]{2,1,0:T(8,128)} %baseline.1) | copy-start | bytes 147460
  25.2 4.0 %collective-permute-start.1 = (f32[3,8,256]{2,0,1:T(4,128)S(1)}, f32[3,8,256]{2,0,1:T(4,128)S(1)}, u32[]{:S(2)}, u32[]{:S(2)}) collective-permute-start(f32[3,8,256]{2,0,1:T(4,128)S(1)} %slice.4), channel_id=1, source_target_pairs={{0,2},{1,3},{2,0},{3,1},{4,6},{5,7},{6,4},{7,5},{8,10},{9,11},{10,... | collective-permute-start | bytes 73736 | tf_op jit(solution)/shard_map/ppermute | solution.py:327
  26.8 2.4 %collective-permute-start.2 = (f32[3,8,256]{2,0,1:T(4,128)S(1)}, f32[3,8,256]{2,0,1:T(4,128)S(1)}, u32[]{:S(2)}, u32[]{:S(2)}) collective-permute-start(f32[3,8,256]{2,0,1:T(4,128)S(1)} %slice.4), channel_id=1, source_target_pairs={{0,1},{1,0},{2,3},{3,2},{4,5},{5,4},{6,7},{7,6},{8,9},{9,8},{10,11... | collective-permute-start | bytes 73736 | tf_op jit(solution)/shard_map/ppermute | solution.py:327
  26.8 3.4 %collective-permute-start.3 = (f32[3,8,256]{2,0,1:T(4,128)S(1)}, f32[3,8,256]{2,0,1:T(4,128)S(1)}, u32[]{:S(2)}, u32[]{:S(2)}) collective-permute-start(f32[3,8,256]{2,0,1:T(4,128)S(1)} %slice.4), channel_id=1, source_target_pairs={{0,3},{1,2},{2,1},{3,0},{4,7},{5,6},{6,5},{7,4},{8,11},{9,10},{10,... | collective-permute-start | bytes 73736 | tf_op jit(solution)/shard_map/ppermute | solution.py:327
where the time goes:
time: 31.3 us; the launch traced here: 30.9 us
  Pallas kernels  16.2 us (52%)
  starting transfers between devices  7.36 us (24%)
  local copies, waits for them, and re-layouts  4.5 us (14%)
  waiting for transfers between devices  2.57 us (8%)
    pallas_call x1, Pallas kernels, body(): pl.pallas_call(far_kernel(rows, half, channels, width), out_shape=(*weigh...  8.7 us
    pallas_call x1, Pallas kernels, body(): pl.pallas_call(near_kernel(rows, half, channels, width), out_shape=shape(...  6.73 us
    ppermute x1, starting transfers between devices, body(): halo = lax.ppermute(send, ('space', 'step'), pairs)  4.89 us
    unnamed x14, local copies, waits for them, and re-layouts  3.84 us
    ppermute x3, waiting for transfers between devices, partner(): return lax.ppermute(y, 'step', [(i, i ^ k) for i in range(step_n)])  2.55 us
    ppermute x3, starting transfers between devices, partner(): return lax.ppermute(y, 'step', [(i, i ^ k) for i in range(step_n)])  2.47 us
    pallas_call x1, Pallas kernels, body(): pl.pallas_call(pack_kernel(rows), out_shape=(shape((8, rows, width), F32)...  0.76 us
    div x1, local copies, waits for them, and re-layouts, body(): return difference * whole / step_n  0.63 us
  transfers between devices with their start and end apart: 4, of which 2 were waited for; matrix products, arithmetic and copies ran while one was open for 0% of the time, Pallas kernels for 28%

commit v1 on v0

--- a/solution.py
+++ b/solution.py
@@ -8,6 +8,7 @@
 F32, BF16 = jnp.float32, jnp.bfloat16
 HALO_X, HALO_T = 6, 4
 VMEM = pl.BlockSpec(memory_space=pltpu.VMEM)
+HBM = pl.BlockSpec(memory_space=pltpu.HBM)
 SMEM = pl.BlockSpec(memory_space=pltpu.SMEM)
 
 
@@ -74,8 +75,6 @@
         taps = jnp.concatenate([shift_cols(x, 1), x, shift_cols(x, -1)], 0)
         high = taps.astype(BF16).astype(F32)
         xs[j - x_base] = jnp.concatenate([high, taps - high], 0).astype(BF16)
-    for j in rows("t"):
-        t.put(0, j, t_row(j))
     for j in rows("a1"):
         stack = xs[j - 1 - x_base : j + 2 - x_base].reshape(3 * xs.shape[1], width)
         pre = dot(w1[...], jnp.concatenate([stack, stack], 0))
@@ -90,6 +89,8 @@
             a2.put(s, j, keep(act, j))
             if inside("s2", j):
                 s2[s, j - s2_base] = keep(slope, j)
+    for j in rows("t"):
+        t.put(0, j, t_row(j))
     for j in rows("d3"):
         grad = combine(t.conv(wb[2], 0, j), channels)
         for s in range(2):
@@ -145,13 +146,21 @@
 
 
 def pack_kernel(rows):
-    def kernel(side_ref, fractions, image, baseline, target, x_own, send, tile, sem):
+    def kernel(side_ref, fractions, image, baseline, target, x_own, send, image_copy, base_copy, sems, row_sems):
         side = side_ref[0]
         channels = target.shape[0]
-        start = pl.multiple_of((1 - side) * (rows - 8), 8)
-        fetch = pltpu.make_async_copy(target.at[:, pl.ds(start, 8), :], tile, sem)
-        fetch.start()
-        base, difference = baseline[...], image[...] - baseline[...]
+        copies = []
+        for source, landing, i in ((image, image_copy, 0), (baseline, base_copy, 1)):
+            copies.append(pltpu.make_async_copy(source, landing, sems.at[i]))
+            copies[-1].start()
+        for j in range(HALO_T):
+            row = jnp.where(side == 0, rows - HALO_T + j, HALO_T - 1 - j)
+            place = send.at[pl.ds(channels * j, channels), :]
+            copies.append(pltpu.make_async_copy(target.at[:, row, :], place, row_sems.at[j]))
+            copies[-1].start()
+        copies[0].wait()
+        copies[1].wait()
+        base, difference = base_copy[...], image_copy[...] - base_copy[...]
         colours = base.shape[0]
         zero = jnp.zeros((4 - colours,) + base.shape[1:], F32)
         for s in range(2):
@@ -160,10 +169,8 @@
         for j in range(HALO_X):
             row = jnp.where(side == 0, rows - HALO_X + j, HALO_X - 1 - j)
             send[pl.ds(HALO_T * channels + 8 * j, 8), :] = x_own[:, row, :]
-        fetch.wait()
-        for j in range(HALO_T):
-            row = jnp.where(side == 0, 8 - HALO_T + j, HALO_T - 1 - j)
-            send[pl.ds(channels * j, channels), :] = tile[:, row, :]
+        for copy in copies[2:]:
+            copy.wait()
 
     return kernel
 
@@ -176,15 +183,33 @@
     return near, far
 
 
+def fetch_rows(target, landing, sems, row_of, span):
+    copies = {}
+    for i, local in enumerate(range(span[0], span[1] + 1)):
+        copies[local] = pltpu.make_async_copy(target.at[:, row_of(local), :], landing.at[i], sems.at[i])
+        copies[local].start()
+
+    def t_row(local):
+        copies[local].wait()
+        return landing[local - span[0]]
+
+    return t_row
+
+
 def far_kernel(rows, half, channels, width):
     def kernel(side_ref, x_own, target, w, w_first, *refs):
         w1, wf, wb, w1t, out = refs[:5]
         edges, (e1, e2) = refs[5:15], refs[15:17]
         xs, s1, s2 = refs[17:20]
-        work = refs[20:]
+        w_copy, t_rows, w_sem, t_sems = refs[20:24]
+        work = refs[24:]
         side = side_ref[0]
         row_of = lambda local: jnp.where(side == 0, local, rows - 1 - local)
-        prepare(side, w, w_first, w1, wf, wb, w1t, channels, x_colours(w_first))
+        w_fetch = pltpu.make_async_copy(w, w_copy, w_sem)
+        w_fetch.start()
+        t_row = fetch_rows(target, t_rows, t_sems, row_of, spans_of(half)[1]["t"])
+        w_fetch.wait()
+        prepare(side, w_copy, w_first, w1, wf, wb, w1t, channels, x_colours(w_first))
         spans = spans_of(half)[1]
         maps = [Maps(work[2 * i : 2 * i + 2], b) for i, b in enumerate((1, 2, 2, 3, 4, 5))]
 
@@ -193,7 +218,7 @@
 
         run(
             spans, (w1, wf, wb, w1t), xs, 0, maps, (s1, 1, s2, 2),
-            lambda j: x_own[:, row_of(j), :], lambda j: target[:, row_of(j), :],
+            lambda j: x_own[:, row_of(j), :], t_row,
             lambda value, j: value, emit, channels, width,
         )
         a1, a2, _, d3, d2, d1 = maps
@@ -215,10 +240,12 @@
         edges, (e1, e2) = refs[5:15], refs[15:17]
         out = refs[17]
         xs, s1, s2 = refs[18:21]
-        work = refs[21:]
+        t_rows, t_sems = refs[21:23]
+        work = refs[23:]
         side, exists = info[0], info[1] == 1
         row_of = lambda local: jnp.where(side == 0, local, rows - 1 - local)
         place = lambda local: jnp.where(side == 0, local, half - 1 - local)
+        own_t_row = fetch_rows(target, t_rows, t_sems, row_of, (0, spans_of(half)[0]["t"][1]))
         spans = spans_of(half)[0]
         maps = [Maps(work[2 * i : 2 * i + 2], b) for i, b in enumerate((-5, -4, -4, -3, -2, -1))]
         a1, a2, _, d3, d2, d1 = maps
@@ -237,7 +264,7 @@
         def t_row(j):
             if j < 0:
                 return halo[pl.ds(channels * (j + HALO_T), channels), :]
-            return target[:, row_of(j), :]
+            return own_t_row(j)
 
         def keep(value, j):
             return jnp.where(exists, value, 0.0) if j < 0 else value
@@ -264,18 +291,22 @@
     fractions = jnp.stack([first / step_n, (first + 1.0) / step_n])
     exists = jnp.where(side == 0, space > 0, space < space_n - 1)
     info = jnp.stack([side, exists.astype(jnp.int32)]).astype(jnp.int32)
+    in_hbm = lambda array: pltpu.with_memory_space_constraint(array, pltpu.HBM)
+    target_hbm = in_hbm(target)
+    w_hbm = in_hbm(w_rest.transpose(0, 3, 4, 1, 2))
     params = pltpu.CompilerParams(vmem_limit_bytes=40 << 20)
     shape = jax.ShapeDtypeStruct
 
     x_own, send = pl.pallas_call(
         pack_kernel(rows),
         out_shape=(shape((8, rows, width), F32), shape((HALO_T * channels + HALO_X * 8, width), F32)),
-        in_specs=[SMEM, SMEM, VMEM, VMEM, pl.BlockSpec(memory_space=pl.ANY)],
+        in_specs=[SMEM, SMEM, HBM, HBM, HBM],
         out_specs=(VMEM, VMEM),
-        scratch_shapes=[pltpu.VMEM((channels, 8, width), F32), pltpu.SemaphoreType.DMA(())],
+        scratch_shapes=[pltpu.VMEM((colours, rows, width), F32)] * 2
+        + [pltpu.SemaphoreType.DMA((2,)), pltpu.SemaphoreType.DMA((HALO_T,))],
         compiler_params=params,
         name="pack_edges",
-    )(info, fractions, image, baseline, target)
+    )(info, fractions, in_hbm(image), in_hbm(baseline), target_hbm)
 
     pairs = []
     for i in range(space_n):
@@ -295,9 +326,12 @@
     edge_shapes = [shape((2, 2, channels, width), BF16)] * 10
     edge_shapes += [shape((2, 4, channels, width), F32), shape((2, 2, channels, width), F32)]
 
-    def scratch(x_rows, s1_rows, s2_rows, counts):
+    def scratch(x_rows, s1_rows, s2_rows, t_rows, counts, weights=False):
         refs = [pltpu.VMEM((x_rows, 48, width), BF16)]
         refs += [pltpu.VMEM((2, r, channels, width), F32) for r in (s1_rows, s2_rows)]
+        refs += [pltpu.VMEM((3, 3, 3, channels, channels), F32)] * weights
+        refs += [pltpu.VMEM((t_rows, channels, width), F32)]
+        refs += [pltpu.SemaphoreType.DMA(())] * weights + [pltpu.SemaphoreType.DMA((t_rows,))]
         for i, count in enumerate(counts):
             refs += [pltpu.VMEM((1 if i == 2 else 2, count, channels, width), BF16)] * 2
         return refs
@@ -305,22 +339,22 @@
     far = pl.pallas_call(
         far_kernel(rows, half, channels, width),
         out_shape=(*weight_shapes, shape((half - 6, 8, width), F32), *edge_shapes),
-        in_specs=[SMEM] + [VMEM] * 4,
+        in_specs=[SMEM, VMEM, HBM, HBM, VMEM],
         out_specs=(VMEM,) * 17,
-        scratch_shapes=scratch(half + 6, half, half, (half + 4, half + 2, half + 2, half, half - 2, half - 4)),
+        scratch_shapes=scratch(half + 6, half, half, half + 2, (half + 4, half + 2, half + 2, half, half - 2, half - 4), True),
         compiler_params=params,
         name="far_rows",
-    )(info, x_own, target, w_rest.transpose(0, 3, 4, 1, 2), w_first.transpose(1, 2, 3, 0))
+    )(info, x_own, target_hbm, w_hbm, w_first.transpose(1, 2, 3, 0))
 
     y = pl.pallas_call(
         near_kernel(rows, half, channels, width),
         out_shape=shape((half, 8, width), F32),
-        in_specs=[SMEM] + [VMEM] * 20,
+        in_specs=[SMEM, VMEM, HBM] + [VMEM] * 18,
         out_specs=VMEM,
-        scratch_shapes=scratch(8, 6, 6, (8,) * 6),
+        scratch_shapes=scratch(8, 6, 6, 4, (8,) * 6),
         compiler_params=params,
         name="near_rows",
-    )(info, x_own, target, halo, *far)
+    )(info, x_own, target_hbm, halo, *far)
     y = y.transpose(1, 0, 2)[:colours]
 
     def partner(k):

time: 31.3 us -> 28.4 us (0.907)
  local copies, waits for them, and re-layouts: 4.5 us -> 0.65 us
  Pallas kernels: 16.2 us -> 17.3 us
    unnamed x14 -> x6, local copies, waits for them, and re-layouts: 3.84 us -> 0.02 us
    pallas_call x1, Pallas kernels: 0.76 us -> 1.63 us  [body(): pl.pallas_call(pack_kernel(rows), out_shape=(shape((8, rows, width), F32)...]
  transfers between devices with their start and end apart: 4 -> 4, of which waited for: 2 -> 2; matrix products, arithmetic and copies ran while one was open for 0% -> 0% of each run, Pallas kernels for 28% -> 32%
where the time goes in v1:
time: 28.4 us; the launch traced here: 28.2 us
  Pallas kernels  17.3 us (61%)
  starting transfers between devices  7.33 us (26%)
  waiting for transfers between devices  2.57 us (9%)
  local copies, waits for them, and re-layouts  0.65 us (2%)
    pallas_call x1, Pallas kernels, body(): pl.pallas_call(far_kernel(rows, half, channels, width), out_shape=(*weigh...  9 us
    pallas_call x1, Pallas kernels, body(): pl.pallas_call(near_kernel(rows, half, channels, width), out_shape=shape(...  6.63 us
    ppermute x1, starting transfers between devices, body(): halo = lax.ppermute(send, ('space', 'step'), pairs)  4.89 us
    ppermute x3, waiting for transfers between devices, partner(): return lax.ppermute(y, 'step', [(i, i ^ k) for i in range(step_n)])  2.56 us
    ppermute x3, starting transfers between devices, partner(): return lax.ppermute(y, 'step', [(i, i ^ k) for i in range(step_n)])  2.44 us
    pallas_call x1, Pallas kernels, body(): pl.pallas_call(pack_kernel(rows), out_shape=(shape((8, rows, width), F32)...  1.63 us
    div x1, local copies, waits for them, and re-layouts, body(): return difference * whole / step_n  0.63 us
  transfers between devices with their start and end apart: 4, of which 2 were waited for; matrix products, arithmetic and copies ran while one was open for 0% of the time, Pallas kernels for 32%

profile of v1, /device:TPU:0, one launch (start us, length us, event | category | flops | bytes accessed | tf_op | source)
XLA Modules:
  0.0 28.2 jit_solution(11839189782297569409)
XLA Ops:
  0.0 0.1 pad_add_fusion.side_ref.info
  0.1 0.1 pad_maximum_fusion.fractions
  0.2 0.0 copy-start
  0.2 1.6 %pack_edges.1 = (f32[8,16,256]{2,1,0:T(8,128)S(1)}, f32[304,256]{1,0:T(8,128)S(1)}) custom-call(s32[2]{0:T(128)S(1)} %pad_add_fusion.side_ref.info, f32[2]{0:T(128)S(1)} %pad_maximum_fusion.fractions, f32[3,16,256]{2,1,0:T(8,128)} %image.1, f32[3,16,256]{2,1,0:T(8,128)} %baseline.1, f32[64,16,256]{2,1,0:T(8,128)} %target.5), custom_call_target="tpu_custom_call" | custom-call | tf_op jit(solution)/shard_map/pack_edges/pallas_call | solution.py:300
  1.8 4.9 %collective-permute-start = (f32[304,256]{1,0:T(8,128)S(1)}, f32[304,256]{1,0:T(8,128)S(1)}, u32[]{:S(2)}, u32[]{:S(2)}) collective-permute-start(f32[304,256]{1,0:T(8,128)S(1)} %get-tuple-element.25), channel_id=1, source_target_pairs={{5,1},{7,3},{0,4},{9,5},{2,6},{11,7},{4,8},{13,9},{6,10},{15,11},{... | collective-permute-start | bytes 933896 | tf_op jit(solution)/shard_map/ppermute | solution.py:317
  6.7 0.0 copy-done
  6.7 9.0 %far_rows.1 = (bf16[128,288]{1,0:T(8,128)(2,1)S(1)}, bf16[2,192,576]{2,1,0:T(8,128)(2,1)S(1)}, bf16[3,192,576]{2,1,0:T(8,128)(2,1)S(1)}, bf16[24,576]{1,0:T(8,12...) custom-call(s32[2]{0:T(128)S(1)} %pad_add_fusion.side_ref.info, ...), custom_call_target="tpu_custom_call" | custom-call | tf_op jit(solution)/shard_map/far_rows/pallas_call | solution.py:339
  15.7 0.0 collective-permute-done.halo
  15.7 0.0 copy-start.2
  15.7 6.6 %near_rows.1 = f32[8,8,256]{2,1,0:T(8,128)S(1)} custom-call(s32[2]{0:T(128)S(1)} %pad_add_fusion.side_ref.info, f32[8,16,256]{2,1,0:T(8,128)S(1)} %get-tuple-element.24.x_own, f32[64,16,256]{2,1,0:T(8,128)} %target.5, f32[304,256]{1,0:T(8,128)S(1)} %collective-permute-done.halo, bf16[128,288]{1,0:T(8,128)(2,1)S(1)} %get-tuple-element.26.refs_0_, ...), custom_call_target="tpu_custom_call" | custom-call | tf_op jit(solution)/shard_map/near_rows/pallas_call | solution.py:349
  22.4 0.0 copy-start.1
  22.4 1.6 %collective-permute-start.1 = (f32[3,8,256]{2,0,1:T(4,128)S(1)}, f32[3,8,256]{2,0,1:T(4,128)S(1)}, u32[]{:S(2)}, u32[]{:S(2)}) collective-permute-start(f32[3,8,256]{2,0,1:T(4,128)S(1)} %slice.4), channel_id=1, source_target_pairs={{0,2},{1,3},{2,0},{3,1},{4,6},{5,7},{6,4},{7,5},{8,10},{9,11},{10,... | collective-permute-start | bytes 73736 | tf_op jit(solution)/shard_map/ppermute | solution.py:361
  23.9 0.0 copy-done.2
  23.9 0.0 copy-done.1
  24.0 0.1 collective-permute-start.2
  24.0 0.8 %collective-permute-start.3 = (f32[3,8,256]{2,0,1:T(4,128)S(1)}, f32[3,8,256]{2,0,1:T(4,128)S(1)}, u32[]{:S(2)}, u32[]{:S(2)}) collective-permute-start(f32[3,8,256]{2,0,1:T(4,128)S(1)} %slice.4), channel_id=1, source_target_pairs={{0,3},{1,2},{2,1},{3,0},{4,7},{5,6},{6,5},{7,4},{8,11},{9,10},{10,... | collective-permute-start | bytes 73736 | tf_op jit(solution)/shard_map/ppermute | solution.py:361
  24.9 1.5 %collective-permute-done.1 = f32[3,8,256]{2,0,1:T(4,128)S(1)} collective-permute-done((f32[3,8,256]{2,0,1:T(4,128)S(1)}, f32[3,8,256]{2,0,1:T(4,128)S(1)}, u32[]{:S(2)}, u32[]{:S(2)}) %collective-permute-start.1) | collective-permute-done | bytes 24608 | tf_op jit(solution)/shard_map/ppermute | solution.py:361
  26.4 0.0 collective-permute-done.2
  26.4 1.1 %collective-permute-done.3 = f32[3,8,256]{2,0,1:T(4,128)S(1)} collective-permute-done((f32[3,8,256]{2,0,1:T(4,128)S(1)}, f32[3,8,256]{2,0,1:T(4,128)S(1)}, u32[]{:S(2)}, u32[]{:S(2)}) %collective-permute-start.3) | collective-permute-done | bytes 24608 | tf_op jit(solution)/shard_map/ppermute | solution.py:361
  27.5 0.1 fusion.1
  27.5 0.6 %copy.10 = f32[3,16,256]{2,1,0:T(8,128)} copy(f32[3,16,256]{2,0,1:T(4,128)S(1)} %fusion.1) | data formatting | bytes 98304 | tf_op jit(solution)/shard_map/div | solution.py:371
  (4 shorter events, 0.0 us)
Async XLA Ops:
  0.2 6.5 %copy-start = (f32[64,3,3,3]{0,3,2,1:T(4,128)S(1)}, f32[64,3,3,3]{0,3,2,1:T(4,128)}, u32[]{:S(2)}) copy-start(f32[64,3,3,3]{0,3,2,1:T(4,128)} %param.7) | copy-start | bytes 20740
  1.8 13.9 %collective-permute-start = (f32[304,256]{1,0:T(8,128)S(1)}, f32[304,256]{1,0:T(8,128)S(1)}, u32[]{:S(2)}, u32[]{:S(2)}) collective-permute-start(f32[304,256]{1,0:T(8,128)S(1)} %get-tuple-element.25), channel_id=1, source_target_pairs={{5,1},{7,3},{0,4},{9,5},{2,6},{11,7},{4,8},{13,9},{6,10},{15,11},{... | collective-permute-start | bytes 933896 | tf_op jit(solution)/shard_map/ppermute | solution.py:317
  15.7 8.2 %copy-start.2 = (f32[3,16,256]{2,1,0:T(8,128)S(1)}, f32[3,16,256]{2,1,0:T(8,128)}, u32[]{:S(2)}) copy-start(f32[3,16,256]{2,1,0:T(8,128)} %baseline.1) | copy-start | bytes 147460
  22.4 1.6 %copy-start.1 = (f32[3,16,256]{2,1,0:T(8,128)S(1)}, f32[3,16,256]{2,1,0:T(8,128)}, u32[]{:S(2)}) copy-start(f32[3,16,256]{2,1,0:T(8,128)} %image.1) | copy-start | bytes 147460
  22.4 4.0 %collective-permute-start.1 = (f32[3,8,256]{2,0,1:T(4,128)S(1)}, f32[3,8,256]{2,0,1:T(4,128)S(1)}, u32[]{:S(2)}, u32[]{:S(2)}) collective-permute-start(f32[3,8,256]{2,0,1:T(4,128)S(1)} %slice.4), channel_id=1, source_target_pairs={{0,2},{1,3},{2,0},{3,1},{4,6},{5,7},{6,4},{7,5},{8,10},{9,11},{10,... | collective-permute-start | bytes 73736 | tf_op jit(solution)/shard_map/ppermute | solution.py:361
  24.0 2.4 %collective-permute-start.2 = (f32[3,8,256]{2,0,1:T(4,128)S(1)}, f32[3,8,256]{2,0,1:T(4,128)S(1)}, u32[]{:S(2)}, u32[]{:S(2)}) collective-permute-start(f32[3,8,256]{2,0,1:T(4,128)S(1)} %slice.4), channel_id=1, source_target_pairs={{0,1},{1,0},{2,3},{3,2},{4,5},{5,4},{6,7},{7,6},{8,9},{9,8},{10,11... | collective-permute-start | bytes 73736 | tf_op jit(solution)/shard_map/ppermute | solution.py:361
  24.0 3.4 %collective-permute-start.3 = (f32[3,8,256]{2,0,1:T(4,128)S(1)}, f32[3,8,256]{2,0,1:T(4,128)S(1)}, u32[]{:S(2)}, u32[]{:S(2)}) collective-permute-start(f32[3,8,256]{2,0,1:T(4,128)S(1)} %slice.4), channel_id=1, source_target_pairs={{0,3},{1,2},{2,1},{3,0},{4,7},{5,6},{6,5},{7,4},{8,11},{9,10},{10,... | collective-permute-start | bytes 73736 | tf_op jit(solution)/shard_map/ppermute | solution.py:361

commit v2 on v1

--- a/solution.py
+++ b/solution.py
@@ -64,7 +64,7 @@
             part[:, row - self.base : row - self.base + count] = ref[...]
 
 
-def run(spans, weights, xs, x_base, maps, slopes, x_row, t_row, keep, emit, channels, width):
+def run(spans, weights, xs, x_base, maps, slopes, x_row, t_row, keep, emit, channels, width, ready=lambda: None):
     w1, wf, wb, w1t = weights
     a1, a2, t, d3, d2, d1 = maps
     s1, s1_base, s2, s2_base = slopes
@@ -83,6 +83,7 @@
             a1.put(s, j, keep(act, j))
             if inside("s1", j):
                 s1[s, j - s1_base] = keep(slope, j)
+    ready()
     for j in rows("a2"):
         for s in range(2):
             act, slope = silu_and_slope(combine(a1.conv(wf[0], s, j), channels))
@@ -106,16 +107,18 @@
         emit(j, combine(d1.conv(w1t[...], 0, j) + d1.conv(w1t[...], 1, j), 8))
 
 
-def prepare(side, w, w_first, w1, wf, wb, w1t, channels, colours):
+def halves(pieces):
+    high = [p.astype(BF16).astype(F32) for p in pieces]
+    return high, [p - h for p, h in zip(pieces, high)]
+
+
+def wide(pieces):
+    high, low = halves(pieces)
+    return jnp.concatenate(high + low + high, 1).astype(BF16)
+
+
+def prepare_rest(side, w, wf, wb, channels):
     tap = lambda dy: jnp.where(side == 1, 2 - dy, dy)
-
-    def halves(pieces):
-        high = [p.astype(BF16).astype(F32) for p in pieces]
-        return high, [p - h for p, h in zip(pieces, high)]
-
-    def wide(pieces):
-        high, low = halves(pieces)
-        return jnp.concatenate(high + low + high, 1).astype(BF16)
 
     for layer in range(wf.shape[0]):
         for dx in range(3):
@@ -124,6 +127,10 @@
         for dx in range(3):
             pieces = [w[layer, tap(2 - dy), 2 - dx].T for dy in range(3)]
             wb[layer, pl.ds(dx * channels, channels), :] = wide(pieces)
+
+
+def prepare_first(side, w_first, w1, w1t, channels, colours):
+    tap = lambda dy: jnp.where(side == 1, 2 - dy, dy)
     zeros = lambda count: jnp.zeros((count, channels), F32)
     for s in range(2):
         fronts, backs = [], []
@@ -183,33 +190,34 @@
     return near, far
 
 
-def fetch_rows(target, landing, sems, row_of, span):
-    copies = {}
-    for i, local in enumerate(range(span[0], span[1] + 1)):
-        copies[local] = pltpu.make_async_copy(target.at[:, row_of(local), :], landing.at[i], sems.at[i])
-        copies[local].start()
-
-    def t_row(local):
-        copies[local].wait()
-        return landing[local - span[0]]
-
-    return t_row
+def fetch_rows(target, landing, sems, row_of):
+    copies = []
+    for local in range(landing.shape[0]):
+        copies.append(pltpu.make_async_copy(target.at[:, row_of(local), :], landing.at[local], sems.at[local]))
+        copies[-1].start()
+    return lambda local: copies[local].wait()
 
 
 def far_kernel(rows, half, channels, width):
     def kernel(side_ref, x_own, target, w, w_first, *refs):
         w1, wf, wb, w1t, out = refs[:5]
         edges, (e1, e2) = refs[5:15], refs[15:17]
-        xs, s1, s2 = refs[17:20]
-        w_copy, t_rows, w_sem, t_sems = refs[20:24]
+        t_rows = refs[17]
+        xs, s1, s2, w_copy, w_sem, t_sems = refs[18:24]
         work = refs[24:]
         side = side_ref[0]
         row_of = lambda local: jnp.where(side == 0, local, rows - 1 - local)
         w_fetch = pltpu.make_async_copy(w, w_copy, w_sem)
         w_fetch.start()
-        t_row = fetch_rows(target, t_rows, t_sems, row_of, spans_of(half)[1]["t"])
-        w_fetch.wait()
-        prepare(side, w_copy, w_first, w1, wf, wb, w1t, channels, x_colours(w_first))
+        t_row = fetch_rows(target, t_rows, t_sems, row_of)
+        prepare_first(side, w_first, w1, w1t, channels, w_first.shape[0])
+
+        def ready():
+            w_fetch.wait()
+            prepare_rest(side, w_copy, wf, wb, channels)
+            for local in range(t_rows.shape[0]):
+                t_row(local)
+
         spans = spans_of(half)[1]
         maps = [Maps(work[2 * i : 2 * i + 2], b) for i, b in enumerate((1, 2, 2, 3, 4, 5))]
 
@@ -218,8 +226,8 @@
 
         run(
             spans, (w1, wf, wb, w1t), xs, 0, maps, (s1, 1, s2, 2),
-            lambda j: x_own[:, row_of(j), :], t_row,
-            lambda value, j: value, emit, channels, width,
+            lambda j: x_own[:, row_of(j), :], lambda j: t_rows[j],
+            lambda value, j: value, emit, channels, width, ready,
         )
         a1, a2, _, d3, d2, d1 = maps
         for i, (m, row) in enumerate(((a1, 1), (a2, 2), (d3, 3), (d2, 4), (d1, 5))):
@@ -230,22 +238,16 @@
     return kernel
 
 
-def x_colours(w_first):
-    return w_first.shape[0]
-
-
 def near_kernel(rows, half, channels, width):
-    def kernel(info, x_own, target, halo, *refs):
+    def kernel(info, x_own, halo, *refs):
         w1, wf, wb, w1t, far_out = refs[:5]
         edges, (e1, e2) = refs[5:15], refs[15:17]
-        out = refs[17]
-        xs, s1, s2 = refs[18:21]
-        t_rows, t_sems = refs[21:23]
-        work = refs[23:]
+        t_rows, out = refs[17:19]
+        xs, s1, s2 = refs[19:22]
+        work = refs[22:]
         side, exists = info[0], info[1] == 1
         row_of = lambda local: jnp.where(side == 0, local, rows - 1 - local)
         place = lambda local: jnp.where(side == 0, local, half - 1 - local)
-        own_t_row = fetch_rows(target, t_rows, t_sems, row_of, (0, spans_of(half)[0]["t"][1]))
         spans = spans_of(half)[0]
         maps = [Maps(work[2 * i : 2 * i + 2], b) for i, b in enumerate((-5, -4, -4, -3, -2, -1))]
         a1, a2, _, d3, d2, d1 = maps
@@ -264,7 +266,7 @@
         def t_row(j):
             if j < 0:
                 return halo[pl.ds(channels * (j + HALO_T), channels), :]
-            return own_t_row(j)
+            return t_rows[j]
 
         def keep(value, j):
             return jnp.where(exists, value, 0.0) if j < 0 else value
@@ -326,22 +328,22 @@
     edge_shapes = [shape((2, 2, channels, width), BF16)] * 10
     edge_shapes += [shape((2, 4, channels, width), F32), shape((2, 2, channels, width), F32)]
 
-    def scratch(x_rows, s1_rows, s2_rows, t_rows, counts, weights=False):
+    def scratch(x_rows, s1_rows, s2_rows, counts, landing=0):
         refs = [pltpu.VMEM((x_rows, 48, width), BF16)]
         refs += [pltpu.VMEM((2, r, channels, width), F32) for r in (s1_rows, s2_rows)]
-        refs += [pltpu.VMEM((3, 3, 3, channels, channels), F32)] * weights
-        refs += [pltpu.VMEM((t_rows, channels, width), F32)]
-        refs += [pltpu.SemaphoreType.DMA(())] * weights + [pltpu.SemaphoreType.DMA((t_rows,))]
+        if landing:
+            refs += [pltpu.VMEM((3, 3, 3, channels, channels), F32)]
+            refs += [pltpu.SemaphoreType.DMA(()), pltpu.SemaphoreType.DMA((landing,))]
         for i, count in enumerate(counts):
             refs += [pltpu.VMEM((1 if i == 2 else 2, count, channels, width), BF16)] * 2
         return refs
 
     far = pl.pallas_call(
         far_kernel(rows, half, channels, width),
-        out_shape=(*weight_shapes, shape((half - 6, 8, width), F32), *edge_shapes),
+        out_shape=(*weight_shapes, shape((half - 6, 8, width), F32), *edge_shapes, shape((half + 4, channels, width), F32)),
         in_specs=[SMEM, VMEM, HBM, HBM, VMEM],
-        out_specs=(VMEM,) * 17,
-        scratch_shapes=scratch(half + 6, half, half, half + 2, (half + 4, half + 2, half + 2, half, half - 2, half - 4), True),
+        out_specs=(VMEM,) * 18,
+        scratch_shapes=scratch(half + 6, half, half, (half + 4, half + 2, half + 2, half, half - 2, half - 4), half + 4),
         compiler_params=params,
         name="far_rows",
     )(info, x_own, target_hbm, w_hbm, w_first.transpose(1, 2, 3, 0))
@@ -349,12 +351,12 @@
     y = pl.pallas_call(
         near_kernel(rows, half, channels, width),
         out_shape=shape((half, 8, width), F32),
-        in_specs=[SMEM, VMEM, HBM] + [VMEM] * 18,
+        in_specs=[SMEM] + [VMEM] * 20,
         out_specs=VMEM,
-        scratch_shapes=scratch(8, 6, 6, 4, (8,) * 6),
+        scratch_shapes=scratch(8, 6, 6, (8,) * 6),
         compiler_params=params,
         name="near_rows",
-    )(info, x_own, target_hbm, halo, *far)
+    )(info, x_own, halo, *far)
     y = y.transpose(1, 0, 2)[:colours]
 
     def partner(k):

time: 28.4 us -> 26.9 us (0.947)
  Pallas kernels: 17.3 us -> 15.8 us
    pallas_call x1, Pallas kernels: 9 us -> 8.16 us  [body(): pl.pallas_call(far_kernel(rows, half, channels, width), out_shape=(*weigh...]
    pallas_call x1, Pallas kernels: 6.63 us -> 5.98 us  [body(): pl.pallas_call(near_kernel(rows, half, channels, width), out_shape=shape(...]
  transfers between devices with their start and end apart: 4 -> 4, of which waited for: 2 -> 2; matrix products, arithmetic and copies ran while one was open for 0% -> 0% of each run, Pallas kernels for 32% -> 31%
where the time goes in v2:
time: 26.9 us; the launch traced here: 26.7 us
  Pallas kernels  15.8 us (59%)
  starting transfers between devices  7.36 us (27%)
  waiting for transfers between devices  2.55 us (9%)
  local copies, waits for them, and re-layouts  0.67 us (2%)
    pallas_call x1, Pallas kernels, body(): pl.pallas_call(far_kernel(rows, half, channels, width), out_shape=(*weigh...  8.16 us
    pallas_call x1, Pallas kernels, body(): pl.pallas_call(near_kernel(rows, half, channels, width), out_shape=shape(...  5.98 us
    ppermute x1, starting transfers between devices, body(): halo = lax.ppermute(send, ('space', 'step'), pairs)  4.89 us
    ppermute x3, waiting for transfers between devices, partner(): return lax.ppermute(y, 'step', [(i, i ^ k) for i in range(step_n)])  2.55 us
    ppermute x3, starting transfers between devices, partner(): return lax.ppermute(y, 'step', [(i, i ^ k) for i in range(step_n)])  2.47 us
    pallas_call x1, Pallas kernels, body(): pl.pallas_call(pack_kernel(rows), out_shape=(shape((8, rows, width), F32)...  1.63 us
    div x1, local copies, waits for them, and re-layouts, body(): return difference * whole / step_n  0.63 us
  transfers between devices with their start and end apart: 4, of which 2 were waited for; matrix products, arithmetic and copies ran while one was open for 0% of the time, Pallas kernels for 31%

profile of v2, /device:TPU:0, one launch (start us, length us, event | category | flops | bytes accessed | tf_op | source)
XLA Modules:
  0.0 26.7 jit_solution(4291082611101386726)
XLA Ops:
  0.0 0.1 pad_add_fusion.side_ref.info
  0.1 0.1 pad_maximum_fusion.fractions
  0.2 0.0 copy-start
  0.2 1.6 %pack_edges.1 = (f32[8,16,256]{2,1,0:T(8,128)S(1)}, f32[304,256]{1,0:T(8,128)S(1)}) custom-call(s32[2]{0:T(128)S(1)} %pad_add_fusion.side_ref.info, f32[2]{0:T(128)S(1)} %pad_maximum_fusion.fractions, f32[3,16,256]{2,1,0:T(8,128)} %image.1, f32[3,16,256]{2,1,0:T(8,128)} %baseline.1, f32[64,16,256]{2,1,0:T(8,128)} %target.3), custom_call_target="tpu_custom_call" | custom-call | tf_op jit(solution)/shard_map/pack_edges/pallas_call | solution.py:302
  1.8 4.9 %collective-permute-start = (f32[304,256]{1,0:T(8,128)S(1)}, f32[304,256]{1,0:T(8,128)S(1)}, u32[]{:S(2)}, u32[]{:S(2)}) collective-permute-start(f32[304,256]{1,0:T(8,128)S(1)} %get-tuple-element.26), channel_id=1, source_target_pairs={{5,1},{7,3},{0,4},{9,5},{2,6},{11,7},{4,8},{13,9},{6,10},{15,11},{... | collective-permute-start | bytes 933896 | tf_op jit(solution)/shard_map/ppermute | solution.py:319
  6.7 0.0 copy-done
  6.7 8.2 %far_rows.1 = (bf16[128,288]{1,0:T(8,128)(2,1)S(1)}, bf16[2,192,576]{2,1,0:T(8,128)(2,1)S(1)}, bf16[3,192,576]{2,1,0:T(8,128)(2,1)S(1)}, bf16[24,576]{1,0:T(8,12...) custom-call(s32[2]{0:T(128)S(1)} %pad_add_fusion.side_ref.info, ...), custom_call_target="tpu_custom_call" | custom-call | tf_op jit(solution)/shard_map/far_rows/pallas_call | solution.py:341
  14.9 0.0 collective-permute-done.halo
  14.9 0.0 copy-start.2
  14.9 6.0 %near_rows.1 = f32[8,8,256]{2,1,0:T(8,128)S(1)} custom-call(s32[2]{0:T(128)S(1)} %pad_add_fusion.side_ref.info, f32[8,16,256]{2,1,0:T(8,128)S(1)} %get-tuple-element.25.x_own, f32[304,256]{1,0:T(8,128)S(1)} %collective-permute-done.halo, bf16[128,288]{1,0:T(8,128)(2,1)S(1)} %get-tuple-element.27.refs_0_, bf16[2,192,576]{2,1,0:T(8,128)(2,1)S(1)} %get-tuple-element.28.refs_1_, ...), custom_call_target="tpu_custom_call" | custom-call | tf_op jit(solution)/shard_map/near_rows/pallas_call | solution.py:351
  20.9 0.0 copy-start.1
  20.9 1.6 %collective-permute-start.1 = (f32[3,8,256]{2,0,1:T(4,128)S(1)}, f32[3,8,256]{2,0,1:T(4,128)S(1)}, u32[]{:S(2)}, u32[]{:S(2)}) collective-permute-start(f32[3,8,256]{2,0,1:T(4,128)S(1)} %slice.4), channel_id=1, source_target_pairs={{0,2},{1,3},{2,0},{3,1},{4,6},{5,7},{6,4},{7,5},{8,10},{9,11},{10,... | collective-permute-start | bytes 73736 | tf_op jit(solution)/shard_map/ppermute | solution.py:363
  22.5 0.0 copy-done.2
  22.5 0.0 copy-done.1
  22.5 0.1 collective-permute-start.2
  22.6 0.8 %collective-permute-start.3 = (f32[3,8,256]{2,0,1:T(4,128)S(1)}, f32[3,8,256]{2,0,1:T(4,128)S(1)}, u32[]{:S(2)}, u32[]{:S(2)}) collective-permute-start(f32[3,8,256]{2,0,1:T(4,128)S(1)} %slice.4), channel_id=1, source_target_pairs={{0,3},{1,2},{2,1},{3,0},{4,7},{5,6},{6,5},{7,4},{8,11},{9,10},{10,... | collective-permute-start | bytes 73736 | tf_op jit(solution)/shard_map/ppermute | solution.py:363
  23.4 1.5 %collective-permute-done.1 = f32[3,8,256]{2,0,1:T(4,128)S(1)} collective-permute-done((f32[3,8,256]{2,0,1:T(4,128)S(1)}, f32[3,8,256]{2,0,1:T(4,128)S(1)}, u32[]{:S(2)}, u32[]{:S(2)}) %collective-permute-start.1) | collective-permute-done | bytes 24608 | tf_op jit(solution)/shard_map/ppermute | solution.py:363
  24.9 0.0 collective-permute-done.2
  24.9 1.1 %collective-permute-done.3 = f32[3,8,256]{2,0,1:T(4,128)S(1)} collective-permute-done((f32[3,8,256]{2,0,1:T(4,128)S(1)}, f32[3,8,256]{2,0,1:T(4,128)S(1)}, u32[]{:S(2)}, u32[]{:S(2)}) %collective-permute-start.3) | collective-permute-done | bytes 24608 | tf_op jit(solution)/shard_map/ppermute | solution.py:363
  26.0 0.1 fusion.1
  26.0 0.6 %copy.10 = f32[3,16,256]{2,1,0:T(8,128)} copy(f32[3,16,256]{2,0,1:T(4,128)S(1)} %fusion.1) | data formatting | bytes 98304 | tf_op jit(solution)/shard_map/div | solution.py:373
  (4 shorter events, 0.1 us)
Async XLA Ops:
  0.2 6.5 %copy-start = (f32[64,3,3,3]{0,3,2,1:T(4,128)S(1)}, f32[64,3,3,3]{0,3,2,1:T(4,128)}, u32[]{:S(2)}) copy-start(f32[64,3,3,3]{0,3,2,1:T(4,128)} %param.7) | copy-start | bytes 20740
  1.8 13.1 %collective-permute-start = (f32[304,256]{1,0:T(8,128)S(1)}, f32[304,256]{1,0:T(8,128)S(1)}, u32[]{:S(2)}, u32[]{:S(2)}) collective-permute-start(f32[304,256]{1,0:T(8,128)S(1)} %get-tuple-element.26), channel_id=1, source_target_pairs={{5,1},{7,3},{0,4},{9,5},{2,6},{11,7},{4,8},{13,9},{6,10},{15,11},{... | collective-permute-start | bytes 933896 | tf_op jit(solution)/shard_map/ppermute | solution.py:319
  14.9 7.6 %copy-start.2 = (f32[3,16,256]{2,1,0:T(8,128)S(1)}, f32[3,16,256]{2,1,0:T(8,128)}, u32[]{:S(2)}) copy-start(f32[3,16,256]{2,1,0:T(8,128)} %baseline.1) | copy-start | bytes 147460
  20.9 1.6 %copy-start.1 = (f32[3,16,256]{2,1,0:T(8,128)S(1)}, f32[3,16,256]{2,1,0:T(8,128)}, u32[]{:S(2)}) copy-start(f32[3,16,256]{2,1,0:T(8,128)} %image.1) | copy-start | bytes 147460
  20.9 4.0 %collective-permute-start.1 = (f32[3,8,256]{2,0,1:T(4,128)S(1)}, f32[3,8,256]{2,0,1:T(4,128)S(1)}, u32[]{:S(2)}, u32[]{:S(2)}) collective-permute-start(f32[3,8,256]{2,0,1:T(4,128)S(1)} %slice.4), channel_id=1, source_target_pairs={{0,2},{1,3},{2,0},{3,1},{4,6},{5,7},{6,4},{7,5},{8,10},{9,11},{10,... | collective-permute-start | bytes 73736 | tf_op jit(solution)/shard_map/ppermute | solution.py:363
  22.5 2.4 %collective-permute-start.2 = (f32[3,8,256]{2,0,1:T(4,128)S(1)}, f32[3,8,256]{2,0,1:T(4,128)S(1)}, u32[]{:S(2)}, u32[]{:S(2)}) collective-permute-start(f32[3,8,256]{2,0,1:T(4,128)S(1)} %slice.4), channel_id=1, source_target_pairs={{0,1},{1,0},{2,3},{3,2},{4,5},{5,4},{6,7},{7,6},{8,9},{9,8},{10,11... | collective-permute-start | bytes 73736 | tf_op jit(solution)/shard_map/ppermute | solution.py:363
  22.6 3.4 %collective-permute-start.3 = (f32[3,8,256]{2,0,1:T(4,128)S(1)}, f32[3,8,256]{2,0,1:T(4,128)S(1)}, u32[]{:S(2)}, u32[]{:S(2)}) collective-permute-start(f32[3,8,256]{2,0,1:T(4,128)S(1)} %slice.4), channel_id=1, source_target_pairs={{0,3},{1,2},{2,1},{3,0},{4,7},{5,6},{6,5},{7,4},{8,11},{9,10},{10,... | collective-permute-start | bytes 73736 | tf_op jit(solution)/shard_map/ppermute | solution.py:363

commit v3 on v2

--- a/solution.py
+++ b/solution.py
@@ -23,9 +23,15 @@
 
 def shift_cols(value, by):
     width = value.shape[-1]
-    col = lax.broadcasted_iota(jnp.int32, value.shape, value.ndim - 1)
-    edge = 0 if by > 0 else width - 1
-    return jnp.where(col == edge, 0.0, pltpu.roll(value, by % width, value.ndim - 1))
+    rolled = pltpu.roll(value, by % width, 1)
+    cut = 128 if by > 0 else width - 128
+    left, right = rolled[:, :cut], rolled[:, cut:]
+    col = lax.broadcasted_iota(jnp.int32, (value.shape[0], 128), 1)
+    if by > 0:
+        left = jnp.where(col == 0, 0.0, left)
+    else:
+        right = jnp.where(col == 127, 0.0, right)
+    return jnp.concatenate([left, right], 1)
 
 
 def combine(y, rows):
@@ -38,38 +44,52 @@
     return act, sig + act * (1.0 - sig)
 
 
-def conv_row(weights, high, low, index):
-    stack = lambda ref: ref[index : index + 3].reshape(3 * ref.shape[1], ref.shape[2])
-    upper, lower = stack(high), stack(low)
-    return dot(weights, jnp.concatenate([upper, upper, lower], 0))
-
-
 class Maps:
-    def __init__(self, refs, base):
-        self.high, self.low = refs
-        self.base = base
+    def __init__(self, quads, rows_ref, base):
+        self.quads, self.rows_ref, self.base = quads, rows_ref, base
+
+    def add(self, step, quad, rows):
+        channels = rows[0].shape[0]
+        first, second, third, fourth = rows
+        sums = (first - third, second + third, third - second, second - fourth)
+        for i, value in enumerate(sums):
+            high, low = split(value)
+            self.quads[step, quad, i, :channels], self.quads[step, quad, i, channels:] = high, low
 
     def put(self, step, row, value):
-        self.high[step, row - self.base], self.low[step, row - self.base] = split(value)
+        at = row - self.base
+        self.rows_ref[step, at] = value
+        if at % 2 and at >= 3:
+            old = [self.rows_ref[step, at - k] for k in (3, 2, 1)]
+            self.add(step, (at - 3) // 2, (*old, value))
+
+    def seal(self, step):
+        last = self.rows_ref.shape[1]
+        self.add(step, last // 2 - 2, [self.rows_ref[step, last - k] for k in (4, 3, 2, 1)])
 
     def conv(self, weights, step, row):
-        return conv_row(weights, self.high.at[step], self.low.at[step], row - 1 - self.base)
-
-    def copy(self, refs, row, count):
-        for part, ref in zip((self.high, self.low), refs):
-            ref[...] = part[:, row - self.base : row - self.base + count]
-
-    def load(self, refs, row, count):
-        for part, ref in zip((self.high, self.low), refs):
-            part[:, row - self.base : row - self.base + count] = ref[...]
-
-
-def run(spans, weights, xs, x_base, maps, slopes, x_row, t_row, keep, emit, channels, width, ready=lambda: None):
+        quad = (row - 1 - self.base) // 2
+        products = []
+        for i in range(4):
+            both = self.quads[step, quad, i]
+            high, low = both[: both.shape[0] // 2], both[both.shape[0] // 2 :]
+            products.append(dot(weights[i], jnp.concatenate([high, high, low], 0)))
+        return products[0] + (products[1] + products[2]), (products[1] - products[2]) - products[3]
+
+
+def run(spans, weights, xs, x_base, maps, slopes, x_row, t_row, keep, emit, channels, width, ready, sealed):
     w1, wf, wb, w1t = weights
     a1, a2, t, d3, d2, d1 = maps
     s1, s1_base, s2, s2_base = slopes
     rows = lambda name: range(spans[name][0], spans[name][1] + 1)
+    pairs = lambda name: range(spans[name][0], spans[name][1] + 1, 2)
     inside = lambda name, row: spans[name][0] <= row <= spans[name][1]
+
+    def seal(m):
+        if sealed:
+            m.seal(0)
+            m.seal(1)
+
     for j in rows("x"):
         x = x_row(j)
         taps = jnp.concatenate([shift_cols(x, 1), x, shift_cols(x, -1)], 0)
@@ -83,28 +103,40 @@
             a1.put(s, j, keep(act, j))
             if inside("s1", j):
                 s1[s, j - s1_base] = keep(slope, j)
+    seal(a1)
     ready()
-    for j in rows("a2"):
-        for s in range(2):
-            act, slope = silu_and_slope(combine(a1.conv(wf[0], s, j), channels))
-            a2.put(s, j, keep(act, j))
-            if inside("s2", j):
-                s2[s, j - s2_base] = keep(slope, j)
-    for j in rows("t"):
-        t.put(0, j, t_row(j))
-    for j in rows("d3"):
-        grad = combine(t.conv(wb[2], 0, j), channels)
-        for s in range(2):
-            _, slope = silu_and_slope(combine(a2.conv(wf[1], s, j), channels))
-            d3.put(s, j, keep(grad * slope, j))
-    for j in rows("d2"):
-        for s in range(2):
-            d2.put(s, j, combine(d3.conv(wb[1], s, j), channels) * s2[s, j - s2_base])
-    for j in rows("d1"):
-        for s in range(2):
-            d1.put(s, j, combine(d2.conv(wb[0], s, j), channels) * s1[s, j - s1_base])
-    for j in rows("out"):
-        emit(j, combine(d1.conv(w1t[...], 0, j) + d1.conv(w1t[...], 1, j), 8))
+    for i in pairs("a2"):
+        for s in range(2):
+            for j, y in zip((i, i + 1), a1.conv(wf.at[0], s, i)):
+                act, slope = silu_and_slope(combine(y, channels))
+                a2.put(s, j, keep(act, j))
+                if inside("s2", j):
+                    s2[s, j - s2_base] = keep(slope, j)
+    seal(a2)
+    for j in pairs("t"):
+        if j + 3 <= spans["t"][1]:
+            t.add(0, (j - t.base) // 2, [t_row(j + k) for k in range(4)])
+    for i in pairs("d3"):
+        grads = [combine(y, channels) for y in t.conv(wb.at[2], 0, i)]
+        for s in range(2):
+            for j, grad, y in zip((i, i + 1), grads, a2.conv(wf.at[1], s, i)):
+                _, slope = silu_and_slope(combine(y, channels))
+                d3.put(s, j, keep(grad * slope, j))
+    seal(d3)
+    for i in pairs("d2"):
+        for s in range(2):
+            for j, y in zip((i, i + 1), d3.conv(wb.at[1], s, i)):
+                d2.put(s, j, combine(y, channels) * s2[s, j - s2_base])
+    seal(d2)
+    for i in pairs("d1"):
+        for s in range(2):
+            for j, y in zip((i, i + 1), d2.conv(wb.at[0], s, i)):
+                d1.put(s, j, combine(y, channels) * s1[s, j - s1_base])
+    seal(d1)
+    for i in pairs("out"):
+        zero, one = (d1.conv(w1t, s, i) for s in range(2))
+        for j, y, z in zip((i, i + 1), zero, one):
+            emit(j, combine(y + z, 8))
 
 
 def halves(pieces):
@@ -117,16 +149,21 @@
     return jnp.concatenate(high + low + high, 1).astype(BF16)
 
 
+def filters(taps):
+    even, odd = 0.5 * (taps[0] + taps[2]), 0.5 * taps[1]
+    return taps[0], even + odd, even - odd, taps[2]
+
+
 def prepare_rest(side, w, wf, wb, channels):
     tap = lambda dy: jnp.where(side == 1, 2 - dy, dy)
-
-    for layer in range(wf.shape[0]):
-        for dx in range(3):
-            wf[layer, pl.ds(dx * channels, channels), :] = wide([w[layer, tap(dy), dx] for dy in range(3)])
-    for layer in range(wb.shape[0]):
-        for dx in range(3):
-            pieces = [w[layer, tap(2 - dy), 2 - dx].T for dy in range(3)]
-            wb[layer, pl.ds(dx * channels, channels), :] = wide(pieces)
+    for dx in range(3):
+        place = pl.ds(dx * channels, channels)
+        for layer in range(wf.shape[0]):
+            for i, piece in enumerate(filters([w[layer, tap(dy), dx] for dy in range(3)])):
+                wf[layer, i, place, :] = wide([piece])
+        for layer in range(wb.shape[0]):
+            for i, piece in enumerate(filters([w[layer, tap(2 - dy), 2 - dx] for dy in range(3)])):
+                wb[layer, i, place, :] = wide([piece.T])
 
 
 def prepare_first(side, w_first, w1, w1t, channels, colours):
@@ -149,7 +186,8 @@
         )
         for dy in range(3)
     ]
-    w1t[...] = wide(last)
+    for i, piece in enumerate(filters(last)):
+        w1t[i] = wide([piece])
 
 
 def pack_kernel(rows):
@@ -198,13 +236,19 @@
     return lambda local: copies[local].wait()
 
 
+def build_maps(work, bases):
+    quads, floats = work[:6], list(work[6:])
+    floats.insert(2, None)
+    return [Maps(q, r, base) for q, r, base in zip(quads, floats, bases)]
+
+
 def far_kernel(rows, half, channels, width):
     def kernel(side_ref, x_own, target, w, w_first, *refs):
         w1, wf, wb, w1t, out = refs[:5]
-        edges, (e1, e2) = refs[5:15], refs[15:17]
-        t_rows = refs[17]
-        xs, s1, s2, w_copy, w_sem, t_sems = refs[18:24]
-        work = refs[24:]
+        edges, (e1, e2) = refs[5:10], refs[10:12]
+        t_rows = refs[12]
+        xs, s1, s2, w_copy, w_sem, t_sems = refs[13:19]
+        work = refs[19:]
         side = side_ref[0]
         row_of = lambda local: jnp.where(side == 0, local, rows - 1 - local)
         w_fetch = pltpu.make_async_copy(w, w_copy, w_sem)
@@ -219,7 +263,7 @@
                 t_row(local)
 
         spans = spans_of(half)[1]
-        maps = [Maps(work[2 * i : 2 * i + 2], b) for i, b in enumerate((1, 2, 2, 3, 4, 5))]
+        maps = build_maps(work, (1, 2, 2, 3, 4, 5))
 
         def emit(j, value):
             out[j - spans["out"][0]] = value
@@ -227,11 +271,10 @@
         run(
             spans, (w1, wf, wb, w1t), xs, 0, maps, (s1, 1, s2, 2),
             lambda j: x_own[:, row_of(j), :], lambda j: t_rows[j],
-            lambda value, j: value, emit, channels, width, ready,
+            lambda value, j: value, emit, channels, width, ready, False,
         )
-        a1, a2, _, d3, d2, d1 = maps
-        for i, (m, row) in enumerate(((a1, 1), (a2, 2), (d3, 3), (d2, 4), (d1, 5))):
-            m.copy(edges[2 * i : 2 * i + 2], row, 2)
+        for m, edge in zip(maps[:2] + maps[3:], edges):
+            edge[...] = m.rows_ref[:, 0:2]
         e1[...] = s1[:, 0:4]
         e2[...] = s2[:, 0:2]
 
@@ -241,18 +284,17 @@
 def near_kernel(rows, half, channels, width):
     def kernel(info, x_own, halo, *refs):
         w1, wf, wb, w1t, far_out = refs[:5]
-        edges, (e1, e2) = refs[5:15], refs[15:17]
-        t_rows, out = refs[17:19]
-        xs, s1, s2 = refs[19:22]
-        work = refs[22:]
+        edges, (e1, e2) = refs[5:10], refs[10:12]
+        t_rows, out = refs[12:14]
+        xs, s1, s2 = refs[14:17]
+        work = refs[17:]
         side, exists = info[0], info[1] == 1
         row_of = lambda local: jnp.where(side == 0, local, rows - 1 - local)
         place = lambda local: jnp.where(side == 0, local, half - 1 - local)
         spans = spans_of(half)[0]
-        maps = [Maps(work[2 * i : 2 * i + 2], b) for i, b in enumerate((-5, -4, -4, -3, -2, -1))]
-        a1, a2, _, d3, d2, d1 = maps
-        for i, (m, row) in enumerate(((a1, 1), (a2, 2), (d3, 3), (d2, 4), (d1, 5))):
-            m.load(edges[2 * i : 2 * i + 2], row, 2)
+        maps = build_maps(work, (-5, -4, -4, -3, -2, -1))
+        for m, edge in zip(maps[:2] + maps[3:], edges):
+            m.rows_ref[:, 6:8] = edge[...]
         s1[:, 2:6] = e1[...]
         s2[:, 4:6] = e2[...]
         for j in range(6, half):
@@ -276,7 +318,7 @@
 
         run(
             spans, (w1, wf, wb, w1t), xs, -6, maps, (s1, -1, s2, -2),
-            x_row, t_row, keep, emit, channels, width,
+            x_row, t_row, keep, emit, channels, width, lambda: None, True,
         )
 
     return kernel
@@ -321,11 +363,11 @@
     n = 3 * channels
     weight_shapes = [
         shape((2 * channels, 288), BF16),
-        shape((2, n, 3 * n), BF16),
-        shape((3, n, 3 * n), BF16),
-        shape((24, 3 * n), BF16),
+        shape((2, 4, n, n), BF16),
+        shape((3, 4, n, n), BF16),
+        shape((4, 24, n), BF16),
     ]
-    edge_shapes = [shape((2, 2, channels, width), BF16)] * 10
+    edge_shapes = [shape((2, 2, channels, width), F32)] * 5
     edge_shapes += [shape((2, 4, channels, width), F32), shape((2, 2, channels, width), F32)]
 
     def scratch(x_rows, s1_rows, s2_rows, counts, landing=0):
@@ -335,14 +377,15 @@
             refs += [pltpu.VMEM((3, 3, 3, channels, channels), F32)]
             refs += [pltpu.SemaphoreType.DMA(()), pltpu.SemaphoreType.DMA((landing,))]
         for i, count in enumerate(counts):
-            refs += [pltpu.VMEM((1 if i == 2 else 2, count, channels, width), BF16)] * 2
+            refs += [pltpu.VMEM((1 if i == 2 else 2, count // 2 - 1, 4, 2 * channels, width), BF16)]
+        refs += [pltpu.VMEM((2, count, channels, width), F32) for i, count in enumerate(counts) if i != 2]
         return refs
 
     far = pl.pallas_call(
         far_kernel(rows, half, channels, width),
         out_shape=(*weight_shapes, shape((half - 6, 8, width), F32), *edge_shapes, shape((half + 4, channels, width), F32)),
         in_specs=[SMEM, VMEM, HBM, HBM, VMEM],
-        out_specs=(VMEM,) * 18,
+        out_specs=(VMEM,) * 13,
         scratch_shapes=scratch(half + 6, half, half, (half + 4, half + 2, half + 2, half, half - 2, half - 4), half + 4),
         compiler_params=params,
         name="far_rows",
@@ -351,7 +394,7 @@
     y = pl.pallas_call(
         near_kernel(rows, half, channels, width),
         out_shape=shape((half, 8, width), F32),
-        in_specs=[SMEM] + [VMEM] * 20,
+        in_specs=[SMEM] + [VMEM] * 15,
         out_specs=VMEM,
         scratch_shapes=scratch(8, 6, 6, (8,) * 6),
         compiler_params=params,

time: 26.9 us -> 28 us (1.041)
  Pallas kernels: 15.8 us -> 16.9 us
    pallas_call x1, Pallas kernels: 8.16 us -> 8.9 us  [body(): pl.pallas_call(far_kernel(rows, half, channels, width), out_shape=(*weigh...]
    pallas_call x1, Pallas kernels: 5.98 us -> 6.41 us  [body(): pl.pallas_call(near_kernel(rows, half, channels, width), out_shape=shape(...]
  transfers between devices with their start and end apart: 4 -> 4, of which waited for: 2 -> 2; matrix products, arithmetic and copies ran while one was open for 0% -> 0% of each run, Pallas kernels for 31% -> 32%
where the time goes in v3:
time: 28 us; the launch traced here: 27.8 us
  Pallas kernels  16.9 us (60%)
  starting transfers between devices  7.17 us (26%)
  waiting for transfers between devices  2.74 us (10%)
  local copies, waits for them, and re-layouts  0.65 us (2%)
    pallas_call x1, Pallas kernels, body(): pl.pallas_call(far_kernel(rows, half, channels, width), out_shape=(*weigh...  8.9 us
    pallas_call x1, Pallas kernels, body(): pl.pallas_call(near_kernel(rows, half, channels, width), out_shape=shape(...  6.41 us
    ppermute x1, starting transfers between devices, body(): halo = lax.ppermute(send, ('space', 'step'), pairs)  4.89 us
    ppermute x3, waiting for transfers between devices, partner(): return lax.ppermute(y, 'step', [(i, i ^ k) for i in range(step_n)])  2.74 us
    ppermute x3, starting transfers between devices, partner(): return lax.ppermute(y, 'step', [(i, i ^ k) for i in range(step_n)])  2.28 us
    pallas_call x1, Pallas kernels, body(): pl.pallas_call(pack_kernel(rows), out_shape=(shape((8, rows, width), F32)...  1.63 us
    div x1, local copies, waits for them, and re-layouts, body(): return difference * whole / step_n  0.63 us
  transfers between devices with their start and end apart: 4, of which 2 were waited for; matrix products, arithmetic and copies ran while one was open for 0% of the time, Pallas kernels for 32%

profile of v3, /device:TPU:0, one launch (start us, length us, event | category | flops | bytes accessed | tf_op | source)
XLA Modules:
  0.0 27.8 jit_solution(5812883903581822624)
XLA Ops:
  0.0 0.0 copy-start
  0.0 0.1 pad_add_fusion.side_ref.info
  0.1 0.1 pad_maximum_fusion.fractions
  0.2 1.6 %pack_edges.1 = (f32[8,16,256]{2,1,0:T(8,128)S(1)}, f32[304,256]{1,0:T(8,128)S(1)}) custom-call(s32[2]{0:T(128)S(1)} %pad_add_fusion.side_ref.info, f32[2]{0:T(128)S(1)} %pad_maximum_fusion.fractions, f32[3,16,256]{2,1,0:T(8,128)} %image.1, f32[3,16,256]{2,1,0:T(8,128)} %baseline.1, f32[64,16,256]{2,1,0:T(8,128)} %target.3), custom_call_target="tpu_custom_call" | custom-call | tf_op jit(solution)/shard_map/pack_edges/pallas_call | solution.py:344
  1.8 4.9 %collective-permute-start = (f32[304,256]{1,0:T(8,128)S(1)}, f32[304,256]{1,0:T(8,128)S(1)}, u32[]{:S(2)}, u32[]{:S(2)}) collective-permute-start(f32[304,256]{1,0:T(8,128)S(1)} %get-tuple-element.21), channel_id=1, source_target_pairs={{5,1},{7,3},{0,4},{9,5},{2,6},{11,7},{4,8},{13,9},{6,10},{15,11},{... | collective-permute-start | bytes 933896 | tf_op jit(solution)/shard_map/ppermute | solution.py:361
  6.7 0.0 copy-done
  6.7 8.9 %far_rows.1 = (bf16[128,288]{1,0:T(8,128)(2,1)S(1)}, bf16[2,4,192,192]{3,2,1,0:T(8,128)(2,1)S(1)}, bf16[3,4,192,192]{3,2,1,0:T(8,128)(2,1)S(1)}, bf16[4,24,192]{...) custom-call(s32[2]{0:T(128)S(1)} %pad_add_fusion.side_ref.info, ...), custom_call_target="tpu_custom_call" | custom-call | tf_op jit(solution)/shard_map/far_rows/pallas_call | solution.py:384
  15.6 0.0 collective-permute-done.halo
  15.6 0.0 copy-start.1
  15.6 0.0 copy-start.2
  15.6 6.4 %near_rows.1 = f32[8,8,256]{2,1,0:T(8,128)S(1)} custom-call(s32[2]{0:T(128)S(1)} %pad_add_fusion.side_ref.info, f32[8,16,256]{2,1,0:T(8,128)S(1)} %get-tuple-element.20.x_own, f32[304,256]{1,0:T(8,128)S(1)} %collective-permute-done.halo, bf16[128,288]{1,0:T(8,128)(2,1)S(1)} %get-tuple-element.22.refs_0_, ...), custom_call_target="tpu_custom_call" | custom-call | tf_op jit(solution)/shard_map/near_rows/pallas_call | solution.py:394
  22.1 1.6 %collective-permute-start.1 = (f32[3,8,256]{2,0,1:T(4,128)S(1)}, f32[3,8,256]{2,0,1:T(4,128)S(1)}, u32[]{:S(2)}, u32[]{:S(2)}) collective-permute-start(f32[3,8,256]{2,0,1:T(4,128)S(1)} %slice.4), channel_id=1, source_target_pairs={{0,2},{1,3},{2,0},{3,1},{4,6},{5,7},{6,4},{7,5},{8,10},{9,11},{10,... | collective-permute-start | bytes 73736 | tf_op jit(solution)/shard_map/ppermute | solution.py:406
  23.6 0.0 copy-done.1
  23.6 0.0 copy-done.2
  23.6 0.1 collective-permute-start.2
  23.7 0.6 %collective-permute-start.3 = (f32[3,8,256]{2,0,1:T(4,128)S(1)}, f32[3,8,256]{2,0,1:T(4,128)S(1)}, u32[]{:S(2)}, u32[]{:S(2)}) collective-permute-start(f32[3,8,256]{2,0,1:T(4,128)S(1)} %slice.4), channel_id=1, source_target_pairs={{0,3},{1,2},{2,1},{3,0},{4,7},{5,6},{6,5},{7,4},{8,11},{9,10},{10,... | collective-permute-start | bytes 73736 | tf_op jit(solution)/shard_map/ppermute | solution.py:406
  24.4 1.7 %collective-permute-done.1 = f32[3,8,256]{2,0,1:T(4,128)S(1)} collective-permute-done((f32[3,8,256]{2,0,1:T(4,128)S(1)}, f32[3,8,256]{2,0,1:T(4,128)S(1)}, u32[]{:S(2)}, u32[]{:S(2)}) %collective-permute-start.1) | collective-permute-done | bytes 24608 | tf_op jit(solution)/shard_map/ppermute | solution.py:406
  26.1 0.0 collective-permute-done.2
  26.1 1.1 %collective-permute-done.3 = f32[3,8,256]{2,0,1:T(4,128)S(1)} collective-permute-done((f32[3,8,256]{2,0,1:T(4,128)S(1)}, f32[3,8,256]{2,0,1:T(4,128)S(1)}, u32[]{:S(2)}, u32[]{:S(2)}) %collective-permute-start.3) | collective-permute-done | bytes 24608 | tf_op jit(solution)/shard_map/ppermute | solution.py:406
  27.1 0.1 fusion.1
  27.2 0.6 %copy.10 = f32[3,16,256]{2,1,0:T(8,128)} copy(f32[3,16,256]{2,0,1:T(4,128)S(1)} %fusion.1) | data formatting | bytes 98304 | tf_op jit(solution)/shard_map/div | solution.py:416
  (4 shorter events, 0.0 us)
Async XLA Ops:
  0.0 6.7 %copy-start = (f32[64,3,3,3]{0,3,2,1:T(4,128)S(1)}, f32[64,3,3,3]{0,3,2,1:T(4,128)}, u32[]{:S(2)}) copy-start(f32[64,3,3,3]{0,3,2,1:T(4,128)} %param.7) | copy-start | bytes 20740
  1.8 13.8 %collective-permute-start = (f32[304,256]{1,0:T(8,128)S(1)}, f32[304,256]{1,0:T(8,128)S(1)}, u32[]{:S(2)}, u32[]{:S(2)}) collective-permute-start(f32[304,256]{1,0:T(8,128)S(1)} %get-tuple-element.21), channel_id=1, source_target_pairs={{5,1},{7,3},{0,4},{9,5},{2,6},{11,7},{4,8},{13,9},{6,10},{15,11},{... | collective-permute-start | bytes 933896 | tf_op jit(solution)/shard_map/ppermute | solution.py:361
  15.6 8.0 %copy-start.1 = (f32[3,16,256]{2,1,0:T(8,128)S(1)}, f32[3,16,256]{2,1,0:T(8,128)}, u32[]{:S(2)}) copy-start(f32[3,16,256]{2,1,0:T(8,128)} %image.1) | copy-start | bytes 147460
  15.6 8.0 %copy-start.2 = (f32[3,16,256]{2,1,0:T(8,128)S(1)}, f32[3,16,256]{2,1,0:T(8,128)}, u32[]{:S(2)}) copy-start(f32[3,16,256]{2,1,0:T(8,128)} %baseline.1) | copy-start | bytes 147460
  22.1 4.0 %collective-permute-start.1 = (f32[3,8,256]{2,0,1:T(4,128)S(1)}, f32[3,8,256]{2,0,1:T(4,128)S(1)}, u32[]{:S(2)}, u32[]{:S(2)}) collective-permute-start(f32[3,8,256]{2,0,1:T(4,128)S(1)} %slice.4), channel_id=1, source_target_pairs={{0,2},{1,3},{2,0},{3,1},{4,6},{5,7},{6,4},{7,5},{8,10},{9,11},{10,... | collective-permute-start | bytes 73736 | tf_op jit(solution)/shard_map/ppermute | solution.py:406
  23.6 2.4 %collective-permute-start.2 = (f32[3,8,256]{2,0,1:T(4,128)S(1)}, f32[3,8,256]{2,0,1:T(4,128)S(1)}, u32[]{:S(2)}, u32[]{:S(2)}) collective-permute-start(f32[3,8,256]{2,0,1:T(4,128)S(1)} %slice.4), channel_id=1, source_target_pairs={{0,1},{1,0},{2,3},{3,2},{4,5},{5,4},{6,7},{7,6},{8,9},{9,8},{10,11... | collective-permute-start | bytes 73736 | tf_op jit(solution)/shard_map/ppermute | solution.py:406
  23.7 3.4 %collective-permute-start.3 = (f32[3,8,256]{2,0,1:T(4,128)S(1)}, f32[3,8,256]{2,0,1:T(4,128)S(1)}, u32[]{:S(2)}, u32[]{:S(2)}) collective-permute-start(f32[3,8,256]{2,0,1:T(4,128)S(1)} %slice.4), channel_id=1, source_target_pairs={{0,3},{1,2},{2,1},{3,0},{4,7},{5,6},{6,5},{7,4},{8,11},{9,10},{10,... | collective-permute-start | bytes 73736 | tf_op jit(solution)/shard_map/ppermute | solution.py:406

commit v4 on v2

--- a/solution.py
+++ b/solution.py
@@ -1,3 +1,5 @@
+import functools
+
 import jax
 import jax.numpy as jnp
 from jax import lax
@@ -9,7 +11,6 @@
 HALO_X, HALO_T = 6, 4
 VMEM = pl.BlockSpec(memory_space=pltpu.VMEM)
 HBM = pl.BlockSpec(memory_space=pltpu.HBM)
-SMEM = pl.BlockSpec(memory_space=pltpu.SMEM)
 
 
 def dot(a, b):
@@ -23,9 +24,15 @@
 
 def shift_cols(value, by):
     width = value.shape[-1]
-    col = lax.broadcasted_iota(jnp.int32, value.shape, value.ndim - 1)
-    edge = 0 if by > 0 else width - 1
-    return jnp.where(col == edge, 0.0, pltpu.roll(value, by % width, value.ndim - 1))
+    rolled = pltpu.roll(value, by % width, 1)
+    cut = 128 if by > 0 else width - 128
+    left, right = rolled[:, :cut], rolled[:, cut:]
+    col = lax.broadcasted_iota(jnp.int32, (value.shape[0], 128), 1)
+    if by > 0:
+        left = jnp.where(col == 0, 0.0, left)
+    else:
+        right = jnp.where(col == 127, 0.0, right)
+    return jnp.concatenate([left, right], 1)
 
 
 def combine(y, rows):
@@ -64,7 +71,7 @@
             part[:, row - self.base : row - self.base + count] = ref[...]
 
 
-def run(spans, weights, xs, x_base, maps, slopes, x_row, t_row, keep, emit, channels, width, ready=lambda: None):
+def run(spans, weights, xs, x_base, maps, slopes, x_row, t_row, keep, emit, channels, width, g3=None, ready=None, blocks=()):
     w1, wf, wb, w1t = weights
     a1, a2, t, d3, d2, d1 = maps
     s1, s1_base, s2, s2_base = slopes
@@ -75,7 +82,7 @@
         taps = jnp.concatenate([shift_cols(x, 1), x, shift_cols(x, -1)], 0)
         high = taps.astype(BF16).astype(F32)
         xs[j - x_base] = jnp.concatenate([high, taps - high], 0).astype(BF16)
-    for j in rows("a1"):
+    def first(j):
         stack = xs[j - 1 - x_base : j + 2 - x_base].reshape(3 * xs.shape[1], width)
         pre = dot(w1[...], jnp.concatenate([stack, stack], 0))
         for s in range(2):
@@ -83,17 +90,45 @@
             a1.put(s, j, keep(act, j))
             if inside("s1", j):
                 s1[s, j - s1_base] = keep(slope, j)
-    ready()
-    for j in rows("a2"):
-        for s in range(2):
+
+    def second(j):
+        for s in range(2):
+            if blocks:
+                blocks.pop(0)()
             act, slope = silu_and_slope(combine(a1.conv(wf[0], s, j), channels))
             a2.put(s, j, keep(act, j))
             if inside("s2", j):
                 s2[s, j - s2_base] = keep(slope, j)
-    for j in rows("t"):
-        t.put(0, j, t_row(j))
-    for j in rows("d3"):
-        grad = combine(t.conv(wb[2], 0, j), channels)
+
+    def target_grad(j):
+        return combine(t.conv(wb[2], 0, j), channels)
+
+    def arrive():
+        for j in rows("t"):
+            t.put(0, j, t_row(j))
+
+    firsts, seconds, thirds = list(rows("a1")), list(rows("a2")), list(rows("d3"))
+    early = []
+    if not ready:
+        arrive()
+    for i, j in enumerate(firsts):
+        first(j)
+        if ready and i == 2:
+            ready[0]()
+        if ready and i == 7:
+            ready[1]()
+            arrive()
+        if not ready and thirds[i:]:
+            g3[thirds[i] - thirds[0]] = target_grad(thirds[i])
+            early.append(thirds[i])
+        if i >= 3:
+            second(seconds.pop(0))
+    for j in seconds:
+        second(j)
+    while blocks:
+        blocks.pop(0)()
+    for j in thirds:
+        grad = g3[j - thirds[0]] if j in early else target_grad(j)
         for s in range(2):
             _, slope = silu_and_slope(combine(a2.conv(wf[1], s, j), channels))
             d3.put(s, j, keep(grad * slope, j))
@@ -107,30 +142,29 @@
         emit(j, combine(d1.conv(w1t[...], 0, j) + d1.conv(w1t[...], 1, j), 8))
 
 
-def halves(pieces):
-    high = [p.astype(BF16).astype(F32) for p in pieces]
-    return high, [p - h for p, h in zip(pieces, high)]
-
-
-def wide(pieces):
-    high, low = halves(pieces)
-    return jnp.concatenate(high + low + high, 1).astype(BF16)
-
-
-def prepare_rest(side, w, wf, wb, channels):
-    tap = lambda dy: jnp.where(side == 1, 2 - dy, dy)
-
-    for layer in range(wf.shape[0]):
-        for dx in range(3):
-            wf[layer, pl.ds(dx * channels, channels), :] = wide([w[layer, tap(dy), dx] for dy in range(3)])
-    for layer in range(wb.shape[0]):
-        for dx in range(3):
-            pieces = [w[layer, tap(2 - dy), 2 - dx].T for dy in range(3)]
-            wb[layer, pl.ds(dx * channels, channels), :] = wide(pieces)
-
-
-def prepare_first(side, w_first, w1, w1t, channels, colours):
-    tap = lambda dy: jnp.where(side == 1, 2 - dy, dy)
+def halves(value):
+    high = value.astype(BF16).astype(F32)
+    return high, value - high
+
+
+def wide(value):
+    high, low = halves(value)
+    return jnp.concatenate([high, low, high], 1).astype(BF16)
+
+
+def forward_block(tap, w, wf, layer, dx):
+    channels = w.shape[-1]
+    taps = jnp.concatenate([w[layer, tap(dy), dx] for dy in range(3)], 1)
+    wf[layer, pl.ds(dx * channels, channels), :] = wide(taps)
+
+
+def backward_block(tap, w, wb, layer, dx):
+    channels = w.shape[-1]
+    taps = jnp.concatenate([w[layer, tap(2 - dy), 2 - dx] for dy in range(3)], 0)
+    wb[layer, pl.ds(dx * channels, channels), :] = wide(taps.T)
+
+
+def prepare_first(tap, w_first, w1, w1t, channels, colours):
     zeros = lambda count: jnp.zeros((count, channels), F32)
     for s in range(2):
         fronts, backs = [], []
@@ -139,7 +173,7 @@
                 jnp.concatenate([zeros(4)] * s + [w_first[:, tap(dy), dx, :], zeros(4 - colours)] + [zeros(4)] * (1 - s), 0)
                 for dx in range(3)
             ]
-            (high,), (low,) = halves([jnp.concatenate(slots, 0)])
+            high, low = halves(jnp.concatenate(slots, 0))
             fronts += [high, high]
             backs += [low, jnp.zeros_like(low)]
         w1[pl.ds(s * channels, channels), :] = jnp.concatenate(fronts + backs, 0).T.astype(BF16)
@@ -149,12 +183,18 @@
         )
         for dy in range(3)
     ]
-    w1t[...] = wide(last)
-
-
-def pack_kernel(rows):
-    def kernel(side_ref, fractions, image, baseline, target, x_own, send, image_copy, base_copy, sems, row_sems):
-        side = side_ref[0]
+    w1t[...] = wide(jnp.concatenate(last, 1))
+
+
+def place_on_mesh():
+    step = lax.axis_index("step")
+    return lax.axis_index("space"), lax.rem(step, 2), lax.div(step, 2)
+
+
+def pack_kernel(rows, step_n):
+    def kernel(image, baseline, target, x_own, send, image_copy, base_copy, sems, row_sems):
+        _, side, group = place_on_mesh()
+        fractions = [((2 * group + s).astype(F32) + 0.5) * (1.0 / step_n) for s in range(2)]
         channels = target.shape[0]
         copies = []
         for source, landing, i in ((image, image_copy, 0), (baseline, base_copy, 1)):
@@ -199,24 +239,29 @@
 
 
 def far_kernel(rows, half, channels, width):
-    def kernel(side_ref, x_own, target, w, w_first, *refs):
+    def kernel(x_own, target, w, w_first, *refs):
         w1, wf, wb, w1t, out = refs[:5]
         edges, (e1, e2) = refs[5:15], refs[15:17]
         t_rows = refs[17]
-        xs, s1, s2, w_copy, w_sem, t_sems = refs[18:24]
-        work = refs[24:]
-        side = side_ref[0]
+        xs, s1, s2, t_sems = refs[18:22]
+        work = refs[22:]
+        _, side, _ = place_on_mesh()
         row_of = lambda local: jnp.where(side == 0, local, rows - 1 - local)
-        w_fetch = pltpu.make_async_copy(w, w_copy, w_sem)
-        w_fetch.start()
         t_row = fetch_rows(target, t_rows, t_sems, row_of)
-        prepare_first(side, w_first, w1, w1t, channels, w_first.shape[0])
+        tap = lambda dy: jnp.where(side == 1, 2 - dy, dy)
+        prepare_first(tap, w_first, w1, w1t, channels, w_first.shape[0])
+        backward = lambda layer: [functools.partial(backward_block, tap, w, wb, layer, dx) for dx in range(3)]
+        blocks = backward(0)
 
         def ready():
-            w_fetch.wait()
-            prepare_rest(side, w_copy, wf, wb, channels)
+            for dx in range(3):
+                forward_block(tap, w, wf, 0, dx)
+
+        def landed():
             for local in range(t_rows.shape[0]):
                 t_row(local)
+            blocks.extend(functools.partial(forward_block, tap, w, wf, 1, dx) for dx in range(3))
+            blocks.extend(backward(2) + backward(1))
 
         spans = spans_of(half)[1]
         maps = [Maps(work[2 * i : 2 * i + 2], b) for i, b in enumerate((1, 2, 2, 3, 4, 5))]
@@ -227,7 +272,7 @@
         run(
             spans, (w1, wf, wb, w1t), xs, 0, maps, (s1, 1, s2, 2),
             lambda j: x_own[:, row_of(j), :], lambda j: t_rows[j],
-            lambda value, j: value, emit, channels, width, ready,
+            lambda value, j: value, emit, channels, width, None, (ready, landed), blocks,
         )
         a1, a2, _, d3, d2, d1 = maps
         for i, (m, row) in enumerate(((a1, 1), (a2, 2), (d3, 3), (d2, 4), (d1, 5))):
@@ -238,14 +283,15 @@
     return kernel
 
 
-def near_kernel(rows, half, channels, width):
-    def kernel(info, x_own, halo, *refs):
+def near_kernel(rows, half, channels, width, space_n):
+    def kernel(x_own, halo, *refs):
         w1, wf, wb, w1t, far_out = refs[:5]
         edges, (e1, e2) = refs[5:15], refs[15:17]
         t_rows, out = refs[17:19]
         xs, s1, s2 = refs[19:22]
-        work = refs[22:]
-        side, exists = info[0], info[1] == 1
+        g3, work = refs[22], refs[23:]
+        space, side, _ = place_on_mesh()
+        exists = jnp.where(side == 0, space, space_n - 1 - space) > 0
         row_of = lambda local: jnp.where(side == 0, local, rows - 1 - local)
         place = lambda local: jnp.where(side == 0, local, half - 1 - local)
         spans = spans_of(half)[0]
@@ -276,7 +322,7 @@
 
         run(
             spans, (w1, wf, wb, w1t), xs, -6, maps, (s1, -1, s2, -2),
-            x_row, t_row, keep, emit, channels, width,
+            x_row, t_row, keep, emit, channels, width, g3,
         )
 
     return kernel
@@ -287,28 +333,24 @@
     channels = target.shape[0]
     half = rows // 2
     space_n, step_n = lax.axis_size("space"), lax.axis_size("step")
-    space, step = lax.axis_index("space"), lax.axis_index("step")
-    side, group = step % 2, step // 2
-    first = (group * 2).astype(F32) + 0.5
-    fractions = jnp.stack([first / step_n, (first + 1.0) / step_n])
-    exists = jnp.where(side == 0, space > 0, space < space_n - 1)
-    info = jnp.stack([side, exists.astype(jnp.int32)]).astype(jnp.int32)
+    step = lax.axis_index("step")
+    side = step % 2
     in_hbm = lambda array: pltpu.with_memory_space_constraint(array, pltpu.HBM)
     target_hbm = in_hbm(target)
-    w_hbm = in_hbm(w_rest.transpose(0, 3, 4, 1, 2))
+    w_taps = w_rest.transpose(0, 3, 4, 1, 2)
     params = pltpu.CompilerParams(vmem_limit_bytes=40 << 20)
     shape = jax.ShapeDtypeStruct
 
     x_own, send = pl.pallas_call(
-        pack_kernel(rows),
+        pack_kernel(rows, step_n),
         out_shape=(shape((8, rows, width), F32), shape((HALO_T * channels + HALO_X * 8, width), F32)),
-        in_specs=[SMEM, SMEM, HBM, HBM, HBM],
+        in_specs=[HBM, HBM, HBM],
         out_specs=(VMEM, VMEM),
         scratch_shapes=[pltpu.VMEM((colours, rows, width), F32)] * 2
         + [pltpu.SemaphoreType.DMA((2,)), pltpu.SemaphoreType.DMA((HALO_T,))],
         compiler_params=params,
         name="pack_edges",
-    )(info, fractions, in_hbm(image), in_hbm(baseline), target_hbm)
+    )(in_hbm(image), in_hbm(baseline), target_hbm)
 
     pairs = []
     for i in range(space_n):
@@ -332,8 +374,9 @@
         refs = [pltpu.VMEM((x_rows, 48, width), BF16)]
         refs += [pltpu.VMEM((2, r, channels, width), F32) for r in (s1_rows, s2_rows)]
         if landing:
-            refs += [pltpu.VMEM((3, 3, 3, channels, channels), F32)]
-            refs += [pltpu.SemaphoreType.DMA(()), pltpu.SemaphoreType.DMA((landing,))]
+            refs += [pltpu.SemaphoreType.DMA((landing,))]
+        else:
+            refs += [pltpu.VMEM((6, channels, width), F32)]
         for i, count in enumerate(counts):
             refs += [pltpu.VMEM((1 if i == 2 else 2, count, channels, width), BF16)] * 2
         return refs
@@ -341,22 +384,22 @@
     far = pl.pallas_call(
         far_kernel(rows, half, channels, width),
         out_shape=(*weight_shapes, shape((half - 6, 8, width), F32), *edge_shapes, shape((half + 4, channels, width), F32)),
-        in_specs=[SMEM, VMEM, HBM, HBM, VMEM],
+        in_specs=[VMEM, HBM, VMEM, VMEM],
         out_specs=(VMEM,) * 18,
         scratch_shapes=scratch(half + 6, half, half, (half + 4, half + 2, half + 2, half, half - 2, half - 4), half + 4),
         compiler_params=params,
         name="far_rows",
-    )(info, x_own, target_hbm, w_hbm, w_first.transpose(1, 2, 3, 0))
+    )(x_own, target_hbm, w_taps, w_first.transpose(1, 2, 3, 0))
 
     y = pl.pallas_call(
-        near_kernel(rows, half, channels, width),
+        near_kernel(rows, half, channels, width, space_n),
         out_shape=shape((half, 8, width), F32),
-        in_specs=[SMEM] + [VMEM] * 20,
+        in_specs=[VMEM] * 20,
         out_specs=VMEM,
         scratch_shapes=scratch(8, 6, 6, (8,) * 6),
         compiler_params=params,
         name="near_rows",
-    )(info, x_own, halo, *far)
+    )(x_own, halo, *far)
     y = y.transpose(1, 0, 2)[:colours]
 
     def partner(k):

time: 26.9 us -> 24.9 us (0.926)
  Pallas kernels: 15.8 us -> 13.6 us
  waiting for transfers between devices: 2.55 us -> 2.85 us
    pallas_call x2, Pallas kernels: 7.61 us -> 6.45 us  [the longest x1 5.29 us: body(): pl.pallas_call(near_kernel(rows, half, channels, width, space_n), out_sha...]
    pallas_call x1, Pallas kernels: 8.16 us -> 7.15 us  [body(): pl.pallas_call(far_kernel(rows, half, channels, width), out_shape=(*weigh...]
    ppermute x1, waiting for transfers between devices: 0.01 us -> 0.3 us  [body(): halo = lax.ppermute(send, ('space', 'step'), pairs)]
  transfers between devices with their start and end apart: 4 -> 4, of which waited for: 2 -> 3; matrix products, arithmetic and copies ran while one was open for 0% -> 0% of each run, Pallas kernels for 31% -> 29%
where the time goes in v4:
time: 24.9 us; the launch traced here: 24.6 us
  Pallas kernels  13.6 us (55%)
  starting transfers between devices  7.35 us (30%)
  waiting for transfers between devices  2.85 us (11%)
  local copies, waits for them, and re-layouts  0.67 us (3%)
    pallas_call x1, Pallas kernels, body(): pl.pallas_call(far_kernel(rows, half, channels, width), out_shape=(*weigh...  7.15 us
    pallas_call x1, Pallas kernels, body(): pl.pallas_call(near_kernel(rows, half, channels, width, space_n), out_sha...  5.29 us
    ppermute x1, starting transfers between devices, body(): halo = lax.ppermute(send, ('space', 'step'), pairs)  4.89 us
    ppermute x3, waiting for transfers between devices, partner(): return lax.ppermute(y, 'step', [(i, i ^ k) for i in range(step_n)])  2.55 us
    ppermute x3, starting transfers between devices, partner(): return lax.ppermute(y, 'step', [(i, i ^ k) for i in range(step_n)])  2.46 us
    pallas_call x1, Pallas kernels, body(): pl.pallas_call(pack_kernel(rows, step_n), out_shape=(shape((8, rows, widt...  1.15 us
    div x1, local copies, waits for them, and re-layouts, body(): return difference * whole / step_n  0.63 us
  transfers between devices with their start and end apart: 4, of which 3 were waited for; matrix products, arithmetic and copies ran while one was open for 0% of the time, Pallas kernels for 29%

profile of v4, /device:TPU:0, one launch (start us, length us, event | category | flops | bytes accessed | tf_op | source)
XLA Modules:
  0.0 24.6 jit_solution(12519279805641368866)
XLA Ops:
  0.0 0.0 copy-start
  0.0 0.0 copy-start.1
  0.0 1.2 %pack_edges.1 = (f32[8,16,256]{2,1,0:T(8,128)S(1)}, f32[304,256]{1,0:T(8,128)S(1)}) custom-call(f32[3,16,256]{2,1,0:T(8,128)} %image.1, f32[3,16,256]{2,1,0:T(8,128)} %baseline.1, f32[64,16,256]{2,1,0:T(8,128)} %target.3), custom_call_target="tpu_custom_call" | custom-call | tf_op jit(solution)/shard_map/pack_edges/pallas_call | solution.py:344
  1.2 4.9 %collective-permute-start = (f32[304,256]{1,0:T(8,128)S(1)}, f32[304,256]{1,0:T(8,128)S(1)}, u32[]{:S(2)}, u32[]{:S(2)}) collective-permute-start(f32[304,256]{1,0:T(8,128)S(1)} %get-tuple-element.26), channel_id=1, source_target_pairs={{5,1},{7,3},{0,4},{9,5},{2,6},{11,7},{4,8},{13,9},{6,10},{15,11},{... | collective-permute-start | bytes 933896 | tf_op jit(solution)/shard_map/ppermute | solution.py:361
  6.1 0.0 copy-done
  6.1 0.0 copy-done.1
  6.1 7.2 %far_rows.1 = (bf16[128,288]{1,0:T(8,128)(2,1)S(1)}, bf16[2,192,576]{2,1,0:T(8,128)(2,1)S(1)}, bf16[3,192,576]{2,1,0:T(8,128)(2,1)S(1)}, bf16[24,576]{1,0:T(8,12...) custom-call(f32[8,16,256]{2,1,0:T(8,128)S(1)} %get-tuple-element.25., ...), custom_call_target="tpu_custom_call" | custom-call | tf_op jit(solution)/shard_map/far_rows/pallas_call | solution.py:384
  13.2 0.3 %collective-permute-done.halo = f32[304,256]{1,0:T(8,128)S(1)} collective-permute-done((f32[304,256]{1,0:T(8,128)S(1)}, f32[304,256]{1,0:T(8,128)S(1)}, u32[]{:S(2)}, u32[]{:S(2)}) %collective-permute-start) | collective-permute-done | bytes 311328 | tf_op jit(solution)/shard_map/ppermute | solution.py:361
  13.5 0.0 copy-start.3
  13.5 5.3 %near_rows.1 = f32[8,8,256]{2,1,0:T(8,128)S(1)} custom-call(f32[8,16,256]{2,1,0:T(8,128)S(1)} %get-tuple-element.25.x_own, f32[304,256]{1,0:T(8,128)S(1)} %collective-permute-done.halo, bf16[128,288]{1,0:T(8,128)(2,1)S(1)} %get-tuple-element.27.refs_0_, bf16[2,192,576]{2,1,0:T(8,128)(2,1)S(1)} %get-tuple-element.28.refs_1_, ...), custom_call_target="tpu_custom_call" | custom-call | tf_op jit(solution)/shard_map/near_rows/pallas_call | solution.py:394
  18.8 0.0 copy-start.2
  18.9 1.6 %collective-permute-start.1 = (f32[3,8,256]{2,0,1:T(4,128)S(1)}, f32[3,8,256]{2,0,1:T(4,128)S(1)}, u32[]{:S(2)}, u32[]{:S(2)}) collective-permute-start(f32[3,8,256]{2,0,1:T(4,128)S(1)} %slice.4), channel_id=1, source_target_pairs={{0,2},{1,3},{2,0},{3,1},{4,6},{5,7},{6,4},{7,5},{8,10},{9,11},{10,... | collective-permute-start | bytes 73736 | tf_op jit(solution)/shard_map/ppermute | solution.py:406
  20.4 0.0 copy-done.3
  20.4 0.0 copy-done.2
  20.5 0.1 collective-permute-start.2
  20.5 0.8 %collective-permute-start.3 = (f32[3,8,256]{2,0,1:T(4,128)S(1)}, f32[3,8,256]{2,0,1:T(4,128)S(1)}, u32[]{:S(2)}, u32[]{:S(2)}) collective-permute-start(f32[3,8,256]{2,0,1:T(4,128)S(1)} %slice.4), channel_id=1, source_target_pairs={{0,3},{1,2},{2,1},{3,0},{4,7},{5,6},{6,5},{7,4},{8,11},{9,10},{10,... | collective-permute-start | bytes 73736 | tf_op jit(solution)/shard_map/ppermute | solution.py:406
  21.4 1.5 %collective-permute-done.1 = f32[3,8,256]{2,0,1:T(4,128)S(1)} collective-permute-done((f32[3,8,256]{2,0,1:T(4,128)S(1)}, f32[3,8,256]{2,0,1:T(4,128)S(1)}, u32[]{:S(2)}, u32[]{:S(2)}) %collective-permute-start.1) | collective-permute-done | bytes 24608 | tf_op jit(solution)/shard_map/ppermute | solution.py:406
  22.9 0.0 collective-permute-done.2
  22.9 1.1 %collective-permute-done.3 = f32[3,8,256]{2,0,1:T(4,128)S(1)} collective-permute-done((f32[3,8,256]{2,0,1:T(4,128)S(1)}, f32[3,8,256]{2,0,1:T(4,128)S(1)}, u32[]{:S(2)}, u32[]{:S(2)}) %collective-permute-start.3) | collective-permute-done | bytes 24608 | tf_op jit(solution)/shard_map/ppermute | solution.py:406
  24.0 0.1 fusion.1
  24.0 0.6 %copy.10 = f32[3,16,256]{2,1,0:T(8,128)} copy(f32[3,16,256]{2,0,1:T(4,128)S(1)} %fusion.1) | data formatting | bytes 98304 | tf_op jit(solution)/shard_map/div | solution.py:416
  (4 shorter events, 0.1 us)
Async XLA Ops:
  0.0 6.1 %copy-start = (f32[3,64,64,3,3]{2,1,4,3,0:T(8,128)S(1)}, f32[3,64,64,3,3]{2,1,4,3,0:T(8,128)}, u32[]{:S(2)}) copy-start(f32[3,64,64,3,3]{2,1,4,3,0:T(8,128)} %param.8) | copy-start | bytes 1327108
  0.0 6.1 %copy-start.1 = (f32[64,3,3,3]{0,3,2,1:T(4,128)S(1)}, f32[64,3,3,3]{0,3,2,1:T(4,128)}, u32[]{:S(2)}) copy-start(f32[64,3,3,3]{0,3,2,1:T(4,128)} %param.7) | copy-start | bytes 20740
  1.2 12.4 %collective-permute-start = (f32[304,256]{1,0:T(8,128)S(1)}, f32[304,256]{1,0:T(8,128)S(1)}, u32[]{:S(2)}, u32[]{:S(2)}) collective-permute-start(f32[304,256]{1,0:T(8,128)S(1)} %get-tuple-element.26), channel_id=1, source_target_pairs={{5,1},{7,3},{0,4},{9,5},{2,6},{11,7},{4,8},{13,9},{6,10},{15,11},{... | collective-permute-start | bytes 933896 | tf_op jit(solution)/shard_map/ppermute | solution.py:361
  13.5 6.9 %copy-start.3 = (f32[3,16,256]{2,1,0:T(8,128)S(1)}, f32[3,16,256]{2,1,0:T(8,128)}, u32[]{:S(2)}) copy-start(f32[3,16,256]{2,1,0:T(8,128)} %baseline.1) | copy-start | bytes 147460
  18.8 1.6 %copy-start.2 = (f32[3,16,256]{2,1,0:T(8,128)S(1)}, f32[3,16,256]{2,1,0:T(8,128)}, u32[]{:S(2)}) copy-start(f32[3,16,256]{2,1,0:T(8,128)} %image.1) | copy-start | bytes 147460
  18.9 4.0 %collective-permute-start.1 = (f32[3,8,256]{2,0,1:T(4,128)S(1)}, f32[3,8,256]{2,0,1:T(4,128)S(1)}, u32[]{:S(2)}, u32[]{:S(2)}) collective-permute-start(f32[3,8,256]{2,0,1:T(4,128)S(1)} %slice.4), channel_id=1, source_target_pairs={{0,2},{1,3},{2,0},{3,1},{4,6},{5,7},{6,4},{7,5},{8,10},{9,11},{10,... | collective-permute-start | bytes 73736 | tf_op jit(solution)/shard_map/ppermute | solution.py:406
  20.5 2.4 %collective-permute-start.2 = (f32[3,8,256]{2,0,1:T(4,128)S(1)}, f32[3,8,256]{2,0,1:T(4,128)S(1)}, u32[]{:S(2)}, u32[]{:S(2)}) collective-permute-start(f32[3,8,256]{2,0,1:T(4,128)S(1)} %slice.4), channel_id=1, source_target_pairs={{0,1},{1,0},{2,3},{3,2},{4,5},{5,4},{6,7},{7,6},{8,9},{9,8},{10,11... | collective-permute-start | bytes 73736 | tf_op jit(solution)/shard_map/ppermute | solution.py:406
  20.5 3.4 %collective-permute-start.3 = (f32[3,8,256]{2,0,1:T(4,128)S(1)}, f32[3,8,256]{2,0,1:T(4,128)S(1)}, u32[]{:S(2)}, u32[]{:S(2)}) collective-permute-start(f32[3,8,256]{2,0,1:T(4,128)S(1)} %slice.4), channel_id=1, source_target_pairs={{0,3},{1,2},{2,1},{3,0},{4,7},{5,6},{6,5},{7,4},{8,11},{9,10},{10,... | collective-permute-start | bytes 73736 | tf_op jit(solution)/shard_map/ppermute | solution.py:406

commit v5 on v4

--- a/solution.py
+++ b/solution.py
@@ -136,10 +136,10 @@
         for s in range(2):
             d2.put(s, j, combine(d3.conv(wb[1], s, j), channels) * s2[s, j - s2_base])
     for j in rows("d1"):
-        for s in range(2):
-            d1.put(s, j, combine(d2.conv(wb[0], s, j), channels) * s1[s, j - s1_base])
+        grads = [combine(d2.conv(wb[0], s, j), channels) * s1[s, j - s1_base] for s in range(2)]
+        d1.put(0, j, grads[0] + grads[1])
     for j in rows("out"):
-        emit(j, combine(d1.conv(w1t[...], 0, j) + d1.conv(w1t[...], 1, j), 8))
+        emit(j, combine(d1.conv(w1t[...], 0, j), 8))
 
 
 def halves(value):
@@ -367,7 +367,7 @@
         shape((3, n, 3 * n), BF16),
         shape((24, 3 * n), BF16),
     ]
-    edge_shapes = [shape((2, 2, channels, width), BF16)] * 10
+    edge_shapes = [shape((2, 2, channels, width), BF16)] * 8 + [shape((1, 2, channels, width), BF16)] * 2
     edge_shapes += [shape((2, 4, channels, width), F32), shape((2, 2, channels, width), F32)]
 
     def scratch(x_rows, s1_rows, s2_rows, counts, landing=0):
@@ -378,7 +378,7 @@
         else:
             refs += [pltpu.VMEM((6, channels, width), F32)]
         for i, count in enumerate(counts):
-            refs += [pltpu.VMEM((1 if i == 2 else 2, count, channels, width), BF16)] * 2
+            refs += [pltpu.VMEM((1 if i in (2, 5) else 2, count, channels, width), BF16)] * 2
         return refs
 
     far = pl.pallas_call(
@@ -402,12 +402,13 @@
     )(x_own, halo, *far)
     y = y.transpose(1, 0, 2)[:colours]
 
-    def partner(k):
-        return lax.ppermute(y, "step", [(i, i ^ k) for i in range(step_n)])
+    def partner(value, k):
+        return lax.ppermute(value, "step", [(i, i ^ k) for i in range(step_n)])
 
     difference = image - baseline
     if step_n == 4:
-        mine, theirs = y + partner(2), partner(1) + partner(3)
+        mine = y + partner(y, 2)
+        theirs = partner(mine, 1)
         whole = jnp.where(side == 0, jnp.concatenate([mine, theirs], 1), jnp.concatenate([theirs, mine], 1))
     else:
         order = lax.broadcasted_iota(jnp.int32, (2, 1, 1, 1), 0)

time: 24.9 us -> 24.9 us (level)
  waiting for transfers between devices: 2.85 us -> 3.92 us
  starting transfers between devices: 7.35 us -> 6.52 us
    ppermute x3 -> x2, waiting for transfers between devices: 2.55 us -> 3.57 us  [partner(): return lax.ppermute(value, 'step', [(i, i ^ k) for i in range(step_n)])]
    ppermute x3 -> x2, starting transfers between devices: 2.46 us -> 1.63 us  [partner(): return lax.ppermute(value, 'step', [(i, i ^ k) for i in range(step_n)])]
  transfers between devices with their start and end apart: 4 -> 3, of which waited for: 3 -> 3; matrix products, arithmetic and copies ran while one was open for 0% -> 0% of each run, Pallas kernels for 29% -> 29%
where the time goes in v5:
time: 24.9 us; the launch traced here: 24.8 us
  Pallas kernels  13.5 us (54%)
  starting transfers between devices  6.52 us (26%)
  waiting for transfers between devices  3.92 us (16%)
  local copies, waits for them, and re-layouts  0.67 us (3%)
    pallas_call x1, Pallas kernels, body(): pl.pallas_call(far_kernel(rows, half, channels, width), out_shape=(*weigh...  7.1 us
    pallas_call x1, Pallas kernels, body(): pl.pallas_call(near_kernel(rows, half, channels, width, space_n), out_sha...  5.22 us
    ppermute x1, starting transfers between devices, body(): halo = lax.ppermute(send, ('space', 'step'), pairs)  4.89 us
    ppermute x2, waiting for transfers between devices, partner(): return lax.ppermute(value, 'step', [(i, i ^ k) for i in range(step_n)])  3.57 us
    ppermute x2, starting transfers between devices, partner(): return lax.ppermute(value, 'step', [(i, i ^ k) for i in range(step_n)])  1.63 us
    pallas_call x1, Pallas kernels, body(): pl.pallas_call(pack_kernel(rows, step_n), out_shape=(shape((8, rows, widt...  1.15 us
    div x1, local copies, waits for them, and re-layouts, body(): return difference * whole / step_n  0.63 us
  transfers between devices with their start and end apart: 3, of which 3 were waited for; matrix products, arithmetic and copies ran while one was open for 0% of the time, Pallas kernels for 29%

profile of v5, /device:TPU:0, one launch (start us, length us, event | category | flops | bytes accessed | tf_op | source)
XLA Modules:
  0.0 24.8 jit_solution(10999751362721163438)
XLA Ops:
  0.0 0.0 copy-start
  0.0 0.0 copy-start.1
  0.0 1.2 %pack_edges.1 = (f32[8,16,256]{2,1,0:T(8,128)S(1)}, f32[304,256]{1,0:T(8,128)S(1)}) custom-call(f32[3,16,256]{2,1,0:T(8,128)} %image.1, f32[3,16,256]{2,1,0:T(8,128)} %baseline.1, f32[64,16,256]{2,1,0:T(8,128)} %target.3), custom_call_target="tpu_custom_call" | custom-call | tf_op jit(solution)/shard_map/pack_edges/pallas_call | solution.py:344
  1.2 4.9 %collective-permute-start = (f32[304,256]{1,0:T(8,128)S(1)}, f32[304,256]{1,0:T(8,128)S(1)}, u32[]{:S(2)}, u32[]{:S(2)}) collective-permute-start(f32[304,256]{1,0:T(8,128)S(1)} %get-tuple-element.26), channel_id=1, source_target_pairs={{5,1},{7,3},{0,4},{9,5},{2,6},{11,7},{4,8},{13,9},{6,10},{15,11},{... | collective-permute-start | bytes 933896 | tf_op jit(solution)/shard_map/ppermute | solution.py:361
  6.1 0.0 copy-done
  6.1 0.0 copy-done.1
  6.1 7.1 %far_rows.1 = (bf16[128,288]{1,0:T(8,128)(2,1)S(1)}, bf16[2,192,576]{2,1,0:T(8,128)(2,1)S(1)}, bf16[3,192,576]{2,1,0:T(8,128)(2,1)S(1)}, bf16[24,576]{1,0:T(8,12...) custom-call(f32[8,16,256]{2,1,0:T(8,128)S(1)} %get-tuple-element.25., ...), custom_call_target="tpu_custom_call" | custom-call | tf_op jit(solution)/shard_map/far_rows/pallas_call | solution.py:384
  13.2 0.3 %collective-permute-done.halo = f32[304,256]{1,0:T(8,128)S(1)} collective-permute-done((f32[304,256]{1,0:T(8,128)S(1)}, f32[304,256]{1,0:T(8,128)S(1)}, u32[]{:S(2)}, u32[]{:S(2)}) %collective-permute-start) | collective-permute-done | bytes 311328 | tf_op jit(solution)/shard_map/ppermute | solution.py:361
  13.5 5.2 %near_rows.1 = f32[8,8,256]{2,1,0:T(8,128)S(1)} custom-call(f32[8,16,256]{2,1,0:T(8,128)S(1)} %get-tuple-element.25.x_own, f32[304,256]{1,0:T(8,128)S(1)} %collective-permute-done.halo, bf16[128,288]{1,0:T(8,128)(2,1)S(1)} %get-tuple-element.27.refs_0_, bf16[2,192,576]{2,1,0:T(8,128)(2,1)S(1)} %get-tuple-element.28.refs_1_, ...), custom_call_target="tpu_custom_call" | custom-call | tf_op jit(solution)/shard_map/near_rows/pallas_call | solution.py:394
  18.8 0.0 copy-start.2
  18.8 0.0 copy-start.3
  18.8 1.6 %collective-permute-start.1 = (f32[3,8,256]{2,0,1:T(4,128)S(1)}, f32[3,8,256]{2,0,1:T(4,128)S(1)}, u32[]{:S(2)}, u32[]{:S(2)}) collective-permute-start(f32[3,8,256]{2,0,1:T(4,128)S(1)} %slice.4), channel_id=1, source_target_pairs={{0,2},{1,3},{2,0},{3,1},{4,6},{5,7},{6,4},{7,5},{8,10},{9,11},{10,... | collective-permute-start | bytes 73736 | tf_op jit(solution)/shard_map/ppermute | solution.py:406
  20.4 2.4 %collective-permute-done.1 = f32[3,8,256]{2,0,1:T(4,128)S(1)} collective-permute-done((f32[3,8,256]{2,0,1:T(4,128)S(1)}, f32[3,8,256]{2,0,1:T(4,128)S(1)}, u32[]{:S(2)}, u32[]{:S(2)}) %collective-permute-start.1) | collective-permute-done | bytes 24608 | tf_op jit(solution)/shard_map/ppermute | solution.py:406
  22.8 0.1 collective-permute-start.2
  22.9 0.0 copy-done.2
  22.9 0.0 copy-done.3
  22.9 1.1 %collective-permute-done.2 = f32[3,8,256]{2,0,1:T(4,128)S(1)} collective-permute-done((f32[3,8,256]{2,0,1:T(4,128)S(1)}, f32[3,8,256]{2,0,1:T(4,128)S(1)}, u32[]{:S(2)}, u32[]{:S(2)}) %collective-permute-start.2) | collective-permute-done | bytes 24608 | tf_op jit(solution)/shard_map/ppermute | solution.py:406
  24.1 0.6 %copy.10 = f32[3,16,256]{2,1,0:T(8,128)} copy(f32[3,16,256]{2,0,1:T(4,128)S(1)} %fusion.1) | data formatting | bytes 98304 | tf_op jit(solution)/shard_map/div | solution.py:417
  (4 shorter events, 0.1 us)
Async XLA Ops:
  0.0 6.1 %copy-start = (f32[3,64,64,3,3]{2,1,4,3,0:T(8,128)S(1)}, f32[3,64,64,3,3]{2,1,4,3,0:T(8,128)}, u32[]{:S(2)}) copy-start(f32[3,64,64,3,3]{2,1,4,3,0:T(8,128)} %param.8) | copy-start | bytes 1327108
  0.0 6.1 %copy-start.1 = (f32[64,3,3,3]{0,3,2,1:T(4,128)S(1)}, f32[64,3,3,3]{0,3,2,1:T(4,128)}, u32[]{:S(2)}) copy-start(f32[64,3,3,3]{0,3,2,1:T(4,128)} %param.7) | copy-start | bytes 20740
  1.2 12.4 %collective-permute-start = (f32[304,256]{1,0:T(8,128)S(1)}, f32[304,256]{1,0:T(8,128)S(1)}, u32[]{:S(2)}, u32[]{:S(2)}) collective-permute-start(f32[304,256]{1,0:T(8,128)S(1)} %get-tuple-element.26), channel_id=1, source_target_pairs={{5,1},{7,3},{0,4},{9,5},{2,6},{11,7},{4,8},{13,9},{6,10},{15,11},{... | collective-permute-start | bytes 933896 | tf_op jit(solution)/shard_map/ppermute | solution.py:361
  18.8 4.1 %copy-start.2 = (f32[3,16,256]{2,1,0:T(8,128)S(1)}, f32[3,16,256]{2,1,0:T(8,128)}, u32[]{:S(2)}) copy-start(f32[3,16,256]{2,1,0:T(8,128)} %image.1) | copy-start | bytes 147460
  18.8 4.1 %copy-start.3 = (f32[3,16,256]{2,1,0:T(8,128)S(1)}, f32[3,16,256]{2,1,0:T(8,128)}, u32[]{:S(2)}) copy-start(f32[3,16,256]{2,1,0:T(8,128)} %baseline.1) | copy-start | bytes 147460
  18.8 4.0 %collective-permute-start.1 = (f32[3,8,256]{2,0,1:T(4,128)S(1)}, f32[3,8,256]{2,0,1:T(4,128)S(1)}, u32[]{:S(2)}, u32[]{:S(2)}) collective-permute-start(f32[3,8,256]{2,0,1:T(4,128)S(1)} %slice.4), channel_id=1, source_target_pairs={{0,2},{1,3},{2,0},{3,1},{4,6},{5,7},{6,4},{7,5},{8,10},{9,11},{10,... | collective-permute-start | bytes 73736 | tf_op jit(solution)/shard_map/ppermute | solution.py:406
  22.8 1.3 %collective-permute-start.2 = (f32[3,8,256]{2,0,1:T(4,128)S(1)}, f32[3,8,256]{2,0,1:T(4,128)S(1)}, u32[]{:S(2)}, u32[]{:S(2)}) collective-permute-start(f32[3,8,256]{2,0,1:T(4,128)S(1)} %slice_add_fusion), channel_id=1, source_target_pairs={{0,1},{1,0},{2,3},{3,2},{4,5},{5,4},{6,7},{7,6},{8,9},{9,8},{10,11... | collective-permute-start | bytes 73736 | tf_op jit(solution)/shard_map/ppermute | solution.py:406

commit v6 on v5

--- a/solution.py
+++ b/solution.py
@@ -197,16 +197,16 @@
         fractions = [((2 * group + s).astype(F32) + 0.5) * (1.0 / step_n) for s in range(2)]
         channels = target.shape[0]
         copies = []
-        for source, landing, i in ((image, image_copy, 0), (baseline, base_copy, 1)):
-            copies.append(pltpu.make_async_copy(source, landing, sems.at[i]))
-            copies[-1].start()
         for j in range(HALO_T):
             row = jnp.where(side == 0, rows - HALO_T + j, HALO_T - 1 - j)
             place = send.at[pl.ds(channels * j, channels), :]
             copies.append(pltpu.make_async_copy(target.at[:, row, :], place, row_sems.at[j]))
-            copies[-1].start()
-        copies[0].wait()
-        copies[1].wait()
+        for source, landing, i in ((image, image_copy, 0), (baseline, base_copy, 1)):
+            copies.append(pltpu.make_async_copy(source, landing, sems.at[i]))
+        for copy in copies:
+            copy.start()
+        copies[-2].wait()
+        copies[-1].wait()
         base, difference = base_copy[...], image_copy[...] - base_copy[...]
         colours = base.shape[0]
         zero = jnp.zeros((4 - colours,) + base.shape[1:], F32)
@@ -216,7 +216,7 @@
         for j in range(HALO_X):
             row = jnp.where(side == 0, rows - HALO_X + j, HALO_X - 1 - j)
             send[pl.ds(HALO_T * channels + 8 * j, 8), :] = x_own[:, row, :]
-        for copy in copies[2:]:
+        for copy in copies[:-2]:
             copy.wait()
 
     return kernel
@@ -402,13 +402,12 @@
     )(x_own, halo, *far)
     y = y.transpose(1, 0, 2)[:colours]
 
-    def partner(value, k):
-        return lax.ppermute(value, "step", [(i, i ^ k) for i in range(step_n)])
+    def partner(k):
+        return lax.ppermute(y, "step", [(i, i ^ k) for i in range(step_n)])
 
     difference = image - baseline
     if step_n == 4:
-        mine = y + partner(y, 2)
-        theirs = partner(mine, 1)
+        mine, theirs = y + partner(2), partner(1) + partner(3)
         whole = jnp.where(side == 0, jnp.concatenate([mine, theirs], 1), jnp.concatenate([theirs, mine], 1))
     else:
         order = lax.broadcasted_iota(jnp.int32, (2, 1, 1, 1), 0)

time: 24.9 us -> 24.9 us (level)
  waiting for transfers between devices: 3.92 us -> 2.9 us
  starting transfers between devices: 6.52 us -> 7.34 us
    ppermute x2 -> x3, waiting for transfers between devices: 3.57 us -> 2.55 us  [partner(): return lax.ppermute(y, 'step', [(i, i ^ k) for i in range(step_n)])]
    ppermute x2 -> x3, starting transfers between devices: 1.63 us -> 2.45 us  [partner(): return lax.ppermute(y, 'step', [(i, i ^ k) for i in range(step_n)])]
  transfers between devices with their start and end apart: 3 -> 4, of which waited for: 3 -> 3; matrix products, arithmetic and copies ran while one was open for 0% -> 0% of each run, Pallas kernels for 29% -> 29%
where the time goes in v6:
time: 24.9 us; the launch traced here: 24.6 us
  Pallas kernels  13.5 us (54%)
  starting transfers between devices  7.34 us (29%)
  waiting for transfers between devices  2.9 us (12%)
  local copies, waits for them, and re-layouts  0.67 us (3%)
    pallas_call x1, Pallas kernels, body(): pl.pallas_call(far_kernel(rows, half, channels, width), out_shape=(*weigh...  7.1 us
    pallas_call x1, Pallas kernels, body(): pl.pallas_call(near_kernel(rows, half, channels, width, space_n), out_sha...  5.23 us
    ppermute x1, starting transfers between devices, body(): halo = lax.ppermute(send, ('space', 'step'), pairs)  4.89 us
    ppermute x3, waiting for transfers between devices, partner(): return lax.ppermute(y, 'step', [(i, i ^ k) for i in range(step_n)])  2.55 us
    ppermute x3, starting transfers between devices, partner(): return lax.ppermute(y, 'step', [(i, i ^ k) for i in range(step_n)])  2.45 us
    pallas_call x1, Pallas kernels, body(): pl.pallas_call(pack_kernel(rows, step_n), out_shape=(shape((8, rows, widt...  1.16 us
    div x1, local copies, waits for them, and re-layouts, body(): return difference * whole / step_n  0.63 us
  transfers between devices with their start and end apart: 4, of which 3 were waited for; matrix products, arithmetic and copies ran while one was open for 0% of the time, Pallas kernels for 29%

profile of v6, /device:TPU:0, one launch (start us, length us, event | category | flops | bytes accessed | tf_op | source)
XLA Modules:
  0.0 24.6 jit_solution(6440361098440256931)
XLA Ops:
  0.0 0.0 copy-start
  0.0 0.0 copy-start.1
  0.0 1.2 %pack_edges.1 = (f32[8,16,256]{2,1,0:T(8,128)S(1)}, f32[304,256]{1,0:T(8,128)S(1)}) custom-call(f32[3,16,256]{2,1,0:T(8,128)} %image.1, f32[3,16,256]{2,1,0:T(8,128)} %baseline.1, f32[64,16,256]{2,1,0:T(8,128)} %target.3), custom_call_target="tpu_custom_call" | custom-call | tf_op jit(solution)/shard_map/pack_edges/pallas_call | solution.py:344
  1.2 4.9 %collective-permute-start = (f32[304,256]{1,0:T(8,128)S(1)}, f32[304,256]{1,0:T(8,128)S(1)}, u32[]{:S(2)}, u32[]{:S(2)}) collective-permute-start(f32[304,256]{1,0:T(8,128)S(1)} %get-tuple-element.26), channel_id=1, source_target_pairs={{5,1},{7,3},{0,4},{9,5},{2,6},{11,7},{4,8},{13,9},{6,10},{15,11},{... | collective-permute-start | bytes 933896 | tf_op jit(solution)/shard_map/ppermute | solution.py:361
  6.1 0.0 copy-done
  6.1 0.0 copy-done.1
  6.1 7.1 %far_rows.1 = (bf16[128,288]{1,0:T(8,128)(2,1)S(1)}, bf16[2,192,576]{2,1,0:T(8,128)(2,1)S(1)}, bf16[3,192,576]{2,1,0:T(8,128)(2,1)S(1)}, bf16[24,576]{1,0:T(8,12...) custom-call(f32[8,16,256]{2,1,0:T(8,128)S(1)} %get-tuple-element.25., ...), custom_call_target="tpu_custom_call" | custom-call | tf_op jit(solution)/shard_map/far_rows/pallas_call | solution.py:384
  13.2 0.3 %collective-permute-done.halo = f32[304,256]{1,0:T(8,128)S(1)} collective-permute-done((f32[304,256]{1,0:T(8,128)S(1)}, f32[304,256]{1,0:T(8,128)S(1)}, u32[]{:S(2)}, u32[]{:S(2)}) %collective-permute-start) | collective-permute-done | bytes 311328 | tf_op jit(solution)/shard_map/ppermute | solution.py:361
  13.6 0.0 copy-start.3
  13.6 5.2 %near_rows.1 = f32[8,8,256]{2,1,0:T(8,128)S(1)} custom-call(f32[8,16,256]{2,1,0:T(8,128)S(1)} %get-tuple-element.25.x_own, f32[304,256]{1,0:T(8,128)S(1)} %collective-permute-done.halo, bf16[128,288]{1,0:T(8,128)(2,1)S(1)} %get-tuple-element.27.refs_0_, bf16[2,192,576]{2,1,0:T(8,128)(2,1)S(1)} %get-tuple-element.28.refs_1_, ...), custom_call_target="tpu_custom_call" | custom-call | tf_op jit(solution)/shard_map/near_rows/pallas_call | solution.py:394
  18.8 0.0 copy-start.2
  18.8 1.5 %collective-permute-start.1 = (f32[3,8,256]{2,0,1:T(4,128)S(1)}, f32[3,8,256]{2,0,1:T(4,128)S(1)}, u32[]{:S(2)}, u32[]{:S(2)}) collective-permute-start(f32[3,8,256]{2,0,1:T(4,128)S(1)} %slice.4), channel_id=1, source_target_pairs={{0,2},{1,3},{2,0},{3,1},{4,6},{5,7},{6,4},{7,5},{8,10},{9,11},{10,... | collective-permute-start | bytes 73736 | tf_op jit(solution)/shard_map/ppermute | solution.py:406
  20.4 0.0 copy-done.3
  20.4 0.0 copy-done.2
  20.4 0.1 collective-permute-start.2
  20.5 0.8 %collective-permute-start.3 = (f32[3,8,256]{2,0,1:T(4,128)S(1)}, f32[3,8,256]{2,0,1:T(4,128)S(1)}, u32[]{:S(2)}, u32[]{:S(2)}) collective-permute-start(f32[3,8,256]{2,0,1:T(4,128)S(1)} %slice.4), channel_id=1, source_target_pairs={{0,3},{1,2},{2,1},{3,0},{4,7},{5,6},{6,5},{7,4},{8,11},{9,10},{10,... | collective-permute-start | bytes 73736 | tf_op jit(solution)/shard_map/ppermute | solution.py:406
  21.3 1.5 %collective-permute-done.1 = f32[3,8,256]{2,0,1:T(4,128)S(1)} collective-permute-done((f32[3,8,256]{2,0,1:T(4,128)S(1)}, f32[3,8,256]{2,0,1:T(4,128)S(1)}, u32[]{:S(2)}, u32[]{:S(2)}) %collective-permute-start.1) | collective-permute-done | bytes 24608 | tf_op jit(solution)/shard_map/ppermute | solution.py:406
  22.8 0.0 collective-permute-done.2
  22.8 1.1 %collective-permute-done.3 = f32[3,8,256]{2,0,1:T(4,128)S(1)} collective-permute-done((f32[3,8,256]{2,0,1:T(4,128)S(1)}, f32[3,8,256]{2,0,1:T(4,128)S(1)}, u32[]{:S(2)}, u32[]{:S(2)}) %collective-permute-start.3) | collective-permute-done | bytes 24608 | tf_op jit(solution)/shard_map/ppermute | solution.py:406
  23.9 0.1 fusion.1
  23.9 0.6 %copy.10 = f32[3,16,256]{2,1,0:T(8,128)} copy(f32[3,16,256]{2,0,1:T(4,128)S(1)} %fusion.1) | data formatting | bytes 98304 | tf_op jit(solution)/shard_map/div | solution.py:416
  (4 shorter events, 0.0 us)
Async XLA Ops:
  0.0 6.1 %copy-start = (f32[3,64,64,3,3]{2,1,4,3,0:T(8,128)S(1)}, f32[3,64,64,3,3]{2,1,4,3,0:T(8,128)}, u32[]{:S(2)}) copy-start(f32[3,64,64,3,3]{2,1,4,3,0:T(8,128)} %param.8) | copy-start | bytes 1327108
  0.0 6.1 %copy-start.1 = (f32[64,3,3,3]{0,3,2,1:T(4,128)S(1)}, f32[64,3,3,3]{0,3,2,1:T(4,128)}, u32[]{:S(2)}) copy-start(f32[64,3,3,3]{0,3,2,1:T(4,128)} %param.7) | copy-start | bytes 20740
  1.2 12.4 %collective-permute-start = (f32[304,256]{1,0:T(8,128)S(1)}, f32[304,256]{1,0:T(8,128)S(1)}, u32[]{:S(2)}, u32[]{:S(2)}) collective-permute-start(f32[304,256]{1,0:T(8,128)S(1)} %get-tuple-element.26), channel_id=1, source_target_pairs={{5,1},{7,3},{0,4},{9,5},{2,6},{11,7},{4,8},{13,9},{6,10},{15,11},{... | collective-permute-start | bytes 933896 | tf_op jit(solution)/shard_map/ppermute | solution.py:361
  13.6 6.8 %copy-start.3 = (f32[3,16,256]{2,1,0:T(8,128)S(1)}, f32[3,16,256]{2,1,0:T(8,128)}, u32[]{:S(2)}) copy-start(f32[3,16,256]{2,1,0:T(8,128)} %baseline.1) | copy-start | bytes 147460
  18.8 1.6 %copy-start.2 = (f32[3,16,256]{2,1,0:T(8,128)S(1)}, f32[3,16,256]{2,1,0:T(8,128)}, u32[]{:S(2)}) copy-start(f32[3,16,256]{2,1,0:T(8,128)} %image.1) | copy-start | bytes 147460
  18.8 4.0 %collective-permute-start.1 = (f32[3,8,256]{2,0,1:T(4,128)S(1)}, f32[3,8,256]{2,0,1:T(4,128)S(1)}, u32[]{:S(2)}, u32[]{:S(2)}) collective-permute-start(f32[3,8,256]{2,0,1:T(4,128)S(1)} %slice.4), channel_id=1, source_target_pairs={{0,2},{1,3},{2,0},{3,1},{4,6},{5,7},{6,4},{7,5},{8,10},{9,11},{10,... | collective-permute-start | bytes 73736 | tf_op jit(solution)/shard_map/ppermute | solution.py:406
  20.4 2.4 %collective-permute-start.2 = (f32[3,8,256]{2,0,1:T(4,128)S(1)}, f32[3,8,256]{2,0,1:T(4,128)S(1)}, u32[]{:S(2)}, u32[]{:S(2)}) collective-permute-start(f32[3,8,256]{2,0,1:T(4,128)S(1)} %slice.4), channel_id=1, source_target_pairs={{0,1},{1,0},{2,3},{3,2},{4,5},{5,4},{6,7},{7,6},{8,9},{9,8},{10,11... | collective-permute-start | bytes 73736 | tf_op jit(solution)/shard_map/ppermute | solution.py:406
  20.5 3.4 %collective-permute-start.3 = (f32[3,8,256]{2,0,1:T(4,128)S(1)}, f32[3,8,256]{2,0,1:T(4,128)S(1)}, u32[]{:S(2)}, u32[]{:S(2)}) collective-permute-start(f32[3,8,256]{2,0,1:T(4,128)S(1)} %slice.4), channel_id=1, source_target_pairs={{0,3},{1,2},{2,1},{3,0},{4,7},{5,6},{6,5},{7,4},{8,11},{9,10},{10,... | collective-permute-start | bytes 73736 | tf_op jit(solution)/shard_map/ppermute | solution.py:406

commit v7 on v6

--- a/solution.py
+++ b/solution.py
@@ -215,7 +215,9 @@
             x_own[pl.ds(4 * s + colours, 4 - colours)] = zero
         for j in range(HALO_X):
             row = jnp.where(side == 0, rows - HALO_X + j, HALO_X - 1 - j)
-            send[pl.ds(HALO_T * channels + 8 * j, 8), :] = x_own[:, row, :]
+            for s in range(2):
+                place = HALO_T * channels + (2 * j + s) * colours
+                send[pl.ds(place, colours), :] = x_own[pl.ds(4 * s, colours), row, :]
         for copy in copies[:-2]:
             copy.wait()
 
@@ -283,7 +285,7 @@
     return kernel
 
 
-def near_kernel(rows, half, channels, width, space_n):
+def near_kernel(rows, half, channels, width, space_n, colours):
     def kernel(x_own, halo, *refs):
         w1, wf, wb, w1t, far_out = refs[:5]
         edges, (e1, e2) = refs[5:15], refs[15:17]
@@ -306,7 +308,10 @@
 
         def x_row(j):
             if j < 0:
-                return halo[pl.ds(HALO_T * channels + 8 * (j + HALO_X), 8), :]
+                first = HALO_T * channels + 2 * (j + HALO_X) * colours
+                zero = jnp.zeros((4 - colours, width), F32)
+                pieces = [halo[pl.ds(first + s * colours, colours), :] for s in range(2)]
+                return jnp.concatenate([pieces[0], zero, pieces[1], zero], 0)
             return x_own[:, row_of(j), :]
 
         def t_row(j):
@@ -343,7 +348,7 @@
 
     x_own, send = pl.pallas_call(
         pack_kernel(rows, step_n),
-        out_shape=(shape((8, rows, width), F32), shape((HALO_T * channels + HALO_X * 8, width), F32)),
+        out_shape=(shape((8, rows, width), F32), shape((HALO_T * channels + HALO_X * 2 * colours, width), F32)),
         in_specs=[HBM, HBM, HBM],
         out_specs=(VMEM, VMEM),
         scratch_shapes=[pltpu.VMEM((colours, rows, width), F32)] * 2
@@ -392,7 +397,7 @@
     )(x_own, target_hbm, w_taps, w_first.transpose(1, 2, 3, 0))
 
     y = pl.pallas_call(
-        near_kernel(rows, half, channels, width, space_n),
+        near_kernel(rows, half, channels, width, space_n, colours),
         out_shape=shape((half, 8, width), F32),
         in_specs=[VMEM] * 20,
         out_specs=VMEM,

time: 24.9 us -> 24.7 us (level)
  no operation moved by 1% of the time
where the time goes in v7:
time: 24.7 us; the launch traced here: 24.4 us
  Pallas kernels  13.5 us (55%)
  starting transfers between devices  7.35 us (30%)
  waiting for transfers between devices  2.72 us (11%)
  local copies, waits for them, and re-layouts  0.67 us (3%)
    pallas_call x1, Pallas kernels, body(): pl.pallas_call(far_kernel(rows, half, channels, width), out_shape=(*weigh...  7.11 us
    pallas_call x1, Pallas kernels, body(): pl.pallas_call(near_kernel(rows, half, channels, width, space_n, colours)...  5.25 us
    ppermute x1, starting transfers between devices, body(): halo = lax.ppermute(send, ('space', 'step'), pairs)  4.89 us
    ppermute x3, waiting for transfers between devices, partner(): return lax.ppermute(y, 'step', [(i, i ^ k) for i in range(step_n)])  2.55 us
    ppermute x3, starting transfers between devices, partner(): return lax.ppermute(y, 'step', [(i, i ^ k) for i in range(step_n)])  2.46 us
    pallas_call x1, Pallas kernels, body(): pl.pallas_call(pack_kernel(rows, step_n), out_shape=(shape((8, rows, widt...  1.16 us
    div x1, local copies, waits for them, and re-layouts, body(): return difference * whole / step_n  0.63 us
  transfers between devices with their start and end apart: 4, of which 3 were waited for; matrix products, arithmetic and copies ran while one was open for 0% of the time, Pallas kernels for 29%

profile of v7, /device:TPU:0, one launch (start us, length us, event | category | flops | bytes accessed | tf_op | source)
XLA Modules:
  0.0 24.4 jit_solution(5647957973937606213)
XLA Ops:
  0.0 0.0 copy-start
  0.0 0.0 copy-start.1
  0.0 1.2 %pack_edges.1 = (f32[8,16,256]{2,1,0:T(8,128)S(1)}, f32[292,256]{1,0:T(8,128)S(1)}) custom-call(f32[3,16,256]{2,1,0:T(8,128)} %image.1, f32[3,16,256]{2,1,0:T(8,128)} %baseline.1, f32[64,16,256]{2,1,0:T(8,128)} %target.3), custom_call_target="tpu_custom_call" | custom-call | tf_op jit(solution)/shard_map/pack_edges/pallas_call | solution.py:349
  1.2 4.9 %collective-permute-start = (f32[292,256]{1,0:T(8,128)S(1)}, f32[292,256]{1,0:T(8,128)S(1)}, u32[]{:S(2)}, u32[]{:S(2)}) collective-permute-start(f32[292,256]{1,0:T(8,128)S(1)} %get-tuple-element.26), channel_id=1, source_target_pairs={{5,1},{7,3},{0,4},{9,5},{2,6},{11,7},{4,8},{13,9},{6,10},{15,11},{... | collective-permute-start | bytes 897032 | tf_op jit(solution)/shard_map/ppermute | solution.py:366
  6.1 0.0 copy-done
  6.1 0.0 copy-done.1
  6.1 7.1 %far_rows.1 = (bf16[128,288]{1,0:T(8,128)(2,1)S(1)}, bf16[2,192,576]{2,1,0:T(8,128)(2,1)S(1)}, bf16[3,192,576]{2,1,0:T(8,128)(2,1)S(1)}, bf16[24,576]{1,0:T(8,12...) custom-call(f32[8,16,256]{2,1,0:T(8,128)S(1)} %get-tuple-element.25., ...), custom_call_target="tpu_custom_call" | custom-call | tf_op jit(solution)/shard_map/far_rows/pallas_call | solution.py:389
  13.2 0.2 collective-permute-done.halo
  13.4 0.0 copy-start.3
  13.4 5.2 %near_rows.1 = f32[8,8,256]{2,1,0:T(8,128)S(1)} custom-call(f32[8,16,256]{2,1,0:T(8,128)S(1)} %get-tuple-element.25.x_own, f32[292,256]{1,0:T(8,128)S(1)} %collective-permute-done.halo, bf16[128,288]{1,0:T(8,128)(2,1)S(1)} %get-tuple-element.27.refs_0_, bf16[2,192,576]{2,1,0:T(8,128)(2,1)S(1)} %get-tuple-element.28.refs_1_, ...), custom_call_target="tpu_custom_call" | custom-call | tf_op jit(solution)/shard_map/near_rows/pallas_call | solution.py:399
  18.6 0.0 copy-start.2
  18.7 1.6 %collective-permute-start.1 = (f32[3,8,256]{2,0,1:T(4,128)S(1)}, f32[3,8,256]{2,0,1:T(4,128)S(1)}, u32[]{:S(2)}, u32[]{:S(2)}) collective-permute-start(f32[3,8,256]{2,0,1:T(4,128)S(1)} %slice.4), channel_id=1, source_target_pairs={{0,2},{1,3},{2,0},{3,1},{4,6},{5,7},{6,4},{7,5},{8,10},{9,11},{10,... | collective-permute-start | bytes 73736 | tf_op jit(solution)/shard_map/ppermute | solution.py:411
  20.2 0.0 copy-done.3
  20.2 0.0 copy-done.2
  20.2 0.1 collective-permute-start.2
  20.3 0.8 %collective-permute-start.3 = (f32[3,8,256]{2,0,1:T(4,128)S(1)}, f32[3,8,256]{2,0,1:T(4,128)S(1)}, u32[]{:S(2)}, u32[]{:S(2)}) collective-permute-start(f32[3,8,256]{2,0,1:T(4,128)S(1)} %slice.4), channel_id=1, source_target_pairs={{0,3},{1,2},{2,1},{3,0},{4,7},{5,6},{6,5},{7,4},{8,11},{9,10},{10,... | collective-permute-start | bytes 73736 | tf_op jit(solution)/shard_map/ppermute | solution.py:411
  21.2 1.5 %collective-permute-done.1 = f32[3,8,256]{2,0,1:T(4,128)S(1)} collective-permute-done((f32[3,8,256]{2,0,1:T(4,128)S(1)}, f32[3,8,256]{2,0,1:T(4,128)S(1)}, u32[]{:S(2)}, u32[]{:S(2)}) %collective-permute-start.1) | collective-permute-done | bytes 24608 | tf_op jit(solution)/shard_map/ppermute | solution.py:411
  22.6 0.0 collective-permute-done.2
  22.7 1.1 %collective-permute-done.3 = f32[3,8,256]{2,0,1:T(4,128)S(1)} collective-permute-done((f32[3,8,256]{2,0,1:T(4,128)S(1)}, f32[3,8,256]{2,0,1:T(4,128)S(1)}, u32[]{:S(2)}, u32[]{:S(2)}) %collective-permute-start.3) | collective-permute-done | bytes 24608 | tf_op jit(solution)/shard_map/ppermute | solution.py:411
  23.7 0.1 fusion.1
  23.8 0.6 %copy.10 = f32[3,16,256]{2,1,0:T(8,128)} copy(f32[3,16,256]{2,0,1:T(4,128)S(1)} %fusion.1) | data formatting | bytes 98304 | tf_op jit(solution)/shard_map/div | solution.py:421
  (4 shorter events, 0.0 us)
Async XLA Ops:
  0.0 6.1 %copy-start = (f32[3,64,64,3,3]{2,1,4,3,0:T(8,128)S(1)}, f32[3,64,64,3,3]{2,1,4,3,0:T(8,128)}, u32[]{:S(2)}) copy-start(f32[3,64,64,3,3]{2,1,4,3,0:T(8,128)} %param.8) | copy-start | bytes 1327108
  0.0 6.1 %copy-start.1 = (f32[64,3,3,3]{0,3,2,1:T(4,128)S(1)}, f32[64,3,3,3]{0,3,2,1:T(4,128)}, u32[]{:S(2)}) copy-start(f32[64,3,3,3]{0,3,2,1:T(4,128)} %param.7) | copy-start | bytes 20740
  1.2 12.2 %collective-permute-start = (f32[292,256]{1,0:T(8,128)S(1)}, f32[292,256]{1,0:T(8,128)S(1)}, u32[]{:S(2)}, u32[]{:S(2)}) collective-permute-start(f32[292,256]{1,0:T(8,128)S(1)} %get-tuple-element.26), channel_id=1, source_target_pairs={{5,1},{7,3},{0,4},{9,5},{2,6},{11,7},{4,8},{13,9},{6,10},{15,11},{... | collective-permute-start | bytes 897032 | tf_op jit(solution)/shard_map/ppermute | solution.py:366
  13.4 6.8 %copy-start.3 = (f32[3,16,256]{2,1,0:T(8,128)S(1)}, f32[3,16,256]{2,1,0:T(8,128)}, u32[]{:S(2)}) copy-start(f32[3,16,256]{2,1,0:T(8,128)} %baseline.1) | copy-start | bytes 147460
  18.6 1.6 %copy-start.2 = (f32[3,16,256]{2,1,0:T(8,128)S(1)}, f32[3,16,256]{2,1,0:T(8,128)}, u32[]{:S(2)}) copy-start(f32[3,16,256]{2,1,0:T(8,128)} %image.1) | copy-start | bytes 147460
  18.7 4.0 %collective-permute-start.1 = (f32[3,8,256]{2,0,1:T(4,128)S(1)}, f32[3,8,256]{2,0,1:T(4,128)S(1)}, u32[]{:S(2)}, u32[]{:S(2)}) collective-permute-start(f32[3,8,256]{2,0,1:T(4,128)S(1)} %slice.4), channel_id=1, source_target_pairs={{0,2},{1,3},{2,0},{3,1},{4,6},{5,7},{6,4},{7,5},{8,10},{9,11},{10,... | collective-permute-start | bytes 73736 | tf_op jit(solution)/shard_map/ppermute | solution.py:411
  20.2 2.4 %collective-permute-start.2 = (f32[3,8,256]{2,0,1:T(4,128)S(1)}, f32[3,8,256]{2,0,1:T(4,128)S(1)}, u32[]{:S(2)}, u32[]{:S(2)}) collective-permute-start(f32[3,8,256]{2,0,1:T(4,128)S(1)} %slice.4), channel_id=1, source_target_pairs={{0,1},{1,0},{2,3},{3,2},{4,5},{5,4},{6,7},{7,6},{8,9},{9,8},{10,11... | collective-permute-start | bytes 73736 | tf_op jit(solution)/shard_map/ppermute | solution.py:411
  20.3 3.4 %collective-permute-start.3 = (f32[3,8,256]{2,0,1:T(4,128)S(1)}, f32[3,8,256]{2,0,1:T(4,128)S(1)}, u32[]{:S(2)}, u32[]{:S(2)}) collective-permute-start(f32[3,8,256]{2,0,1:T(4,128)S(1)} %slice.4), channel_id=1, source_target_pairs={{0,3},{1,2},{2,1},{3,0},{4,7},{5,6},{6,5},{7,4},{8,11},{9,10},{10,... | collective-permute-start | bytes 73736 | tf_op jit(solution)/shard_map/ppermute | solution.py:411

commit v8 on v7

--- a/solution.py
+++ b/solution.py
@@ -407,12 +407,13 @@
     )(x_own, halo, *far)
     y = y.transpose(1, 0, 2)[:colours]
 
-    def partner(k):
-        return lax.ppermute(y, "step", [(i, i ^ k) for i in range(step_n)])
+    def partner(value, k):
+        return lax.ppermute(value, "step", [(i, i ^ k) for i in range(step_n)])
 
     difference = image - baseline
     if step_n == 4:
-        mine, theirs = y + partner(2), partner(1) + partner(3)
+        mine = y + partner(y, 2)
+        theirs = partner(mine, 1)
         whole = jnp.where(side == 0, jnp.concatenate([mine, theirs], 1), jnp.concatenate([theirs, mine], 1))
     else:
         order = lax.broadcasted_iota(jnp.int32, (2, 1, 1, 1), 0)

time: 24.7 us -> 24.8 us (level)
  waiting for transfers between devices: 2.72 us -> 3.74 us
  starting transfers between devices: 7.35 us -> 6.52 us
    ppermute x3 -> x2, waiting for transfers between devices: 2.55 us -> 3.57 us  [partner(): return lax.ppermute(value, 'step', [(i, i ^ k) for i in range(step_n)])]
    ppermute x3 -> x2, starting transfers between devices: 2.46 us -> 1.63 us  [partner(): return lax.ppermute(value, 'step', [(i, i ^ k) for i in range(step_n)])]
  transfers between devices with their start and end apart: 4 -> 3, of which waited for: 3 -> 3; matrix products, arithmetic and copies ran while one was open for 0% -> 0% of each run, Pallas kernels for 29% -> 29%
where the time goes in v8:
time: 24.8 us; the launch traced here: 24.6 us
  Pallas kernels  13.5 us (54%)
  starting transfers between devices  6.52 us (26%)
  waiting for transfers between devices  3.74 us (15%)
  local copies, waits for them, and re-layouts  0.67 us (3%)
    pallas_call x1, Pallas kernels, body(): pl.pallas_call(far_kernel(rows, half, channels, width), out_shape=(*weigh...  7.11 us
    pallas_call x1, Pallas kernels, body(): pl.pallas_call(near_kernel(rows, half, channels, width, space_n, colours)...  5.25 us
    ppermute x1, starting transfers between devices, body(): halo = lax.ppermute(send, ('space', 'step'), pairs)  4.89 us
    ppermute x2, waiting for transfers between devices, partner(): return lax.ppermute(value, 'step', [(i, i ^ k) for i in range(step_n)])  3.57 us
    ppermute x2, starting transfers between devices, partner(): return lax.ppermute(value, 'step', [(i, i ^ k) for i in range(step_n)])  1.63 us
    pallas_call x1, Pallas kernels, body(): pl.pallas_call(pack_kernel(rows, step_n), out_shape=(shape((8, rows, widt...  1.16 us
    div x1, local copies, waits for them, and re-layouts, body(): return difference * whole / step_n  0.63 us
  transfers between devices with their start and end apart: 3, of which 3 were waited for; matrix products, arithmetic and copies ran while one was open for 0% of the time, Pallas kernels for 29%

profile of v8, /device:TPU:0, one launch (start us, length us, event | category | flops | bytes accessed | tf_op | source)
XLA Modules:
  0.0 24.6 jit_solution(3692535007309888819)
XLA Ops:
  0.0 0.0 copy-start
  0.0 0.0 copy-start.1
  0.0 1.2 %pack_edges.1 = (f32[8,16,256]{2,1,0:T(8,128)S(1)}, f32[292,256]{1,0:T(8,128)S(1)}) custom-call(f32[3,16,256]{2,1,0:T(8,128)} %image.1, f32[3,16,256]{2,1,0:T(8,128)} %baseline.1, f32[64,16,256]{2,1,0:T(8,128)} %target.3), custom_call_target="tpu_custom_call" | custom-call | tf_op jit(solution)/shard_map/pack_edges/pallas_call | solution.py:349
  1.2 4.9 %collective-permute-start = (f32[292,256]{1,0:T(8,128)S(1)}, f32[292,256]{1,0:T(8,128)S(1)}, u32[]{:S(2)}, u32[]{:S(2)}) collective-permute-start(f32[292,256]{1,0:T(8,128)S(1)} %get-tuple-element.26), channel_id=1, source_target_pairs={{5,1},{7,3},{0,4},{9,5},{2,6},{11,7},{4,8},{13,9},{6,10},{15,11},{... | collective-permute-start | bytes 897032 | tf_op jit(solution)/shard_map/ppermute | solution.py:366
  6.1 0.0 copy-done
  6.1 0.0 copy-done.1
  6.1 7.1 %far_rows.1 = (bf16[128,288]{1,0:T(8,128)(2,1)S(1)}, bf16[2,192,576]{2,1,0:T(8,128)(2,1)S(1)}, bf16[3,192,576]{2,1,0:T(8,128)(2,1)S(1)}, bf16[24,576]{1,0:T(8,12...) custom-call(f32[8,16,256]{2,1,0:T(8,128)S(1)} %get-tuple-element.25., ...), custom_call_target="tpu_custom_call" | custom-call | tf_op jit(solution)/shard_map/far_rows/pallas_call | solution.py:389
  13.2 0.2 collective-permute-done.halo
  13.4 5.2 %near_rows.1 = f32[8,8,256]{2,1,0:T(8,128)S(1)} custom-call(f32[8,16,256]{2,1,0:T(8,128)S(1)} %get-tuple-element.25.x_own, f32[292,256]{1,0:T(8,128)S(1)} %collective-permute-done.halo, bf16[128,288]{1,0:T(8,128)(2,1)S(1)} %get-tuple-element.27.refs_0_, bf16[2,192,576]{2,1,0:T(8,128)(2,1)S(1)} %get-tuple-element.28.refs_1_, ...), custom_call_target="tpu_custom_call" | custom-call | tf_op jit(solution)/shard_map/near_rows/pallas_call | solution.py:399
  18.6 0.0 copy-start.2
  18.7 0.0 copy-start.3
  18.7 1.6 %collective-permute-start.1 = (f32[3,8,256]{2,0,1:T(4,128)S(1)}, f32[3,8,256]{2,0,1:T(4,128)S(1)}, u32[]{:S(2)}, u32[]{:S(2)}) collective-permute-start(f32[3,8,256]{2,0,1:T(4,128)S(1)} %slice.4), channel_id=1, source_target_pairs={{0,2},{1,3},{2,0},{3,1},{4,6},{5,7},{6,4},{7,5},{8,10},{9,11},{10,... | collective-permute-start | bytes 73736 | tf_op jit(solution)/shard_map/ppermute | solution.py:411
  20.2 2.4 %collective-permute-done.1 = f32[3,8,256]{2,0,1:T(4,128)S(1)} collective-permute-done((f32[3,8,256]{2,0,1:T(4,128)S(1)}, f32[3,8,256]{2,0,1:T(4,128)S(1)}, u32[]{:S(2)}, u32[]{:S(2)}) %collective-permute-start.1) | collective-permute-done | bytes 24608 | tf_op jit(solution)/shard_map/ppermute | solution.py:411
  22.7 0.1 collective-permute-start.2
  22.7 0.0 copy-done.2
  22.8 0.0 copy-done.3
  22.8 1.1 %collective-permute-done.2 = f32[3,8,256]{2,0,1:T(4,128)S(1)} collective-permute-done((f32[3,8,256]{2,0,1:T(4,128)S(1)}, f32[3,8,256]{2,0,1:T(4,128)S(1)}, u32[]{:S(2)}, u32[]{:S(2)}) %collective-permute-start.2) | collective-permute-done | bytes 24608 | tf_op jit(solution)/shard_map/ppermute | solution.py:411
  24.0 0.6 %copy.10 = f32[3,16,256]{2,1,0:T(8,128)} copy(f32[3,16,256]{2,0,1:T(4,128)S(1)} %fusion.1) | data formatting | bytes 98304 | tf_op jit(solution)/shard_map/div | solution.py:422
  (4 shorter events, 0.1 us)
Async XLA Ops:
  0.0 6.1 %copy-start = (f32[3,64,64,3,3]{2,1,4,3,0:T(8,128)S(1)}, f32[3,64,64,3,3]{2,1,4,3,0:T(8,128)}, u32[]{:S(2)}) copy-start(f32[3,64,64,3,3]{2,1,4,3,0:T(8,128)} %param.8) | copy-start | bytes 1327108
  0.0 6.1 %copy-start.1 = (f32[64,3,3,3]{0,3,2,1:T(4,128)S(1)}, f32[64,3,3,3]{0,3,2,1:T(4,128)}, u32[]{:S(2)}) copy-start(f32[64,3,3,3]{0,3,2,1:T(4,128)} %param.7) | copy-start | bytes 20740
  1.2 12.2 %collective-permute-start = (f32[292,256]{1,0:T(8,128)S(1)}, f32[292,256]{1,0:T(8,128)S(1)}, u32[]{:S(2)}, u32[]{:S(2)}) collective-permute-start(f32[292,256]{1,0:T(8,128)S(1)} %get-tuple-element.26), channel_id=1, source_target_pairs={{5,1},{7,3},{0,4},{9,5},{2,6},{11,7},{4,8},{13,9},{6,10},{15,11},{... | collective-permute-start | bytes 897032 | tf_op jit(solution)/shard_map/ppermute | solution.py:366
  18.6 4.1 %copy-start.2 = (f32[3,16,256]{2,1,0:T(8,128)S(1)}, f32[3,16,256]{2,1,0:T(8,128)}, u32[]{:S(2)}) copy-start(f32[3,16,256]{2,1,0:T(8,128)} %image.1) | copy-start | bytes 147460
  18.7 4.1 %copy-start.3 = (f32[3,16,256]{2,1,0:T(8,128)S(1)}, f32[3,16,256]{2,1,0:T(8,128)}, u32[]{:S(2)}) copy-start(f32[3,16,256]{2,1,0:T(8,128)} %baseline.1) | copy-start | bytes 147460
  18.7 4.0 %collective-permute-start.1 = (f32[3,8,256]{2,0,1:T(4,128)S(1)}, f32[3,8,256]{2,0,1:T(4,128)S(1)}, u32[]{:S(2)}, u32[]{:S(2)}) collective-permute-start(f32[3,8,256]{2,0,1:T(4,128)S(1)} %slice.4), channel_id=1, source_target_pairs={{0,2},{1,3},{2,0},{3,1},{4,6},{5,7},{6,4},{7,5},{8,10},{9,11},{10,... | collective-permute-start | bytes 73736 | tf_op jit(solution)/shard_map/ppermute | solution.py:411
  22.7 1.3 %collective-permute-start.2 = (f32[3,8,256]{2,0,1:T(4,128)S(1)}, f32[3,8,256]{2,0,1:T(4,128)S(1)}, u32[]{:S(2)}, u32[]{:S(2)}) collective-permute-start(f32[3,8,256]{2,0,1:T(4,128)S(1)} %slice_add_fusion), channel_id=1, source_target_pairs={{0,1},{1,0},{2,3},{3,2},{4,5},{5,4},{6,7},{7,6},{8,9},{9,8},{10,11... | collective-permute-start | bytes 73736 | tf_op jit(solution)/shard_map/ppermute | solution.py:411
